TPU v7x, 32 devices: a whole 2x2x4 slice. The times are simulated.
32 devices in a mesh: gx: 4 (over z), gy: 8 (over y, x, core).
Axes of the slice: x: 2, y: 2, z: 4, core: 2. Of those that a mesh axis runs over, the one named last changes fastest.
Arguments:
- orders: int32 [4, 8, 128], P('gx', 'gy'), may hold values from 3 to 7
- velocity: bfloat16 [4, 8, 3, 512, 128], P('gx', 'gy'), may hold values from -0.29882812 to 0.29882812
- adjoint_field: float32 [4, 8, 3, 512, 128], P('gx', 'gy'), may hold values from -0.3 to 0.3
- face_links: int32 [4, 8, 6, 128], P('gx', 'gy'), may hold values from 0 to 1280, as said below
- orient: int32 [4, 8, 6, 128], P('gx', 'gy'), may hold values from 0 to 3, as said below
- send_faces: int32 [4, 8, 4, 128], P('gx', 'gy'), may hold values from 0 to 768, as said below
Outputs:
- adjoint_image: float32 [4, 8, 3, 512, 128], P('gx', 'gy')
Inputs may be any that keep to these rules, and one draw needn't show every extreme that they name: `face_links`: own face ids, received slots 6 * 128 + k * 128 + s, or the wall column 1280; links are mutual, a face never links to a received slot that its neighbour leaves empty, and faces toward a missing neighbour are walls. `orient`: both sides of a face carry the same orientation. `send_faces`: each own face appears at most once; 768 marks an empty slot; some neighbour pair fills all 128 slots.
All inputs are finite; a program needn't handle non-finite values.
Results may differ from a plain program's by a relative error of at most 0.0003.
Values sent between devices are 32-bit elements; how exact they have to be, the bound alone decides.
No kernel may reach another device: no remote copies, remote signals or barrier semaphores. Data moves between devices by JAX's collectives and lax.ppermute only.
A program may use at most 64 MiB of HBM per device.

v0:
```python
import functools

import jax
import jax.numpy as jnp
import numpy as np
from jax import lax
from jax.experimental import pallas as pl
from jax.experimental.pallas import tpu as pltpu
from jax.sharding import PartitionSpec as P

DELTA = 0.05
BF = jnp.bfloat16
F32 = jnp.float32
SLOPE = [i * (i + 1) / 2.0 for i in range(8)]
MASS = [2.0 / (2.0 * i + 1.0) for i in range(8)]
SYM = [[0, 3, 4], [3, 1, 5], [4, 5, 2]]


def split_np(x):
    hi = np.asarray(x, np.float32).astype(BF)
    lo = np.asarray(x - hi.astype(np.float64), np.float32).astype(BF)
    return hi, lo


@functools.cache
def tables():
    q = np.arange(8)
    x = np.cos(np.pi * (q + 0.5) / 8.0)
    w = np.pi / 8.0 * np.sqrt(1.0 - x * x)
    values, slopes = [np.ones(8), x], [np.zeros(8), np.ones(8)]
    for k in range(1, 7):
        values.append(((2 * k + 1) * x * values[k] - k * values[k - 1]) / (k + 1))
        slopes.append(slopes[k - 1] + (2 * k + 1) * values[k])
    leg, der = np.stack(values, 1), np.stack(slopes, 1)
    grads, divs = [], []
    for par in range(2):
        li, di = leg[:4, par::2], der[:4, par::2]
        full = np.concatenate(
            [
                np.kron(di, np.kron(leg, leg)),
                np.kron(li, np.kron(der, leg)),
                np.kron(li, np.kron(leg, der)),
            ],
            axis=0,
        )
        grads.append(np.concatenate(split_np(full), axis=1))
        divs.append(np.concatenate(split_np(full.T), axis=1))
    sign = (-1.0) ** q
    slope = np.array(SLOPE)
    eye = np.eye(64)
    ztrace = np.concatenate([np.kron(eye, v[None]) for v in (sign, np.ones(8), sign * slope, slope)], 0)
    even = (q % 2 == 0).astype(np.float64)
    odd = 1.0 - even
    zlift = np.concatenate([np.kron(eye, v[:, None]) for v in (even, odd, even * slope, odd * slope)], 1)
    wjk = np.broadcast_to(np.kron(w, w)[:, None], (64, 128))
    mass = np.array(MASS)
    mab = np.broadcast_to(np.kron(mass, mass)[:, None], (64, 128))
    return dict(
        grad=np.stack(grads),
        div=np.stack(divs),
        ztrace=ztrace.astype(BF),
        zlift=zlift.astype(BF),
        wjk=np.asarray(wjk, np.float32),
        mab=np.asarray(mab, np.float32),
        w=[float(v) for v in w],
        wsum=float(np.sum(w) ** 3),
    )


def dot(a, b):
    return jnp.dot(a, b, preferred_element_type=F32)


def split(x):
    hi = x.astype(BF)
    return hi, (x - hi.astype(F32)).astype(BF)


def level():
    row = lax.broadcasted_iota(jnp.int32, (64, 128), 0)
    return jnp.maximum(row // 8, row % 8)


def alive(lev, i, order):
    return jnp.maximum(lev, i) <= order


def masked_split(v_ref, order):
    lev = level()
    parts = [[[], []], [[], []]]
    for i in range(8):
        live = alive(lev, i, order)
        his, los = [], []
        for c in range(3):
            hi, lo = split(jnp.where(live, v_ref[pl.ds(c * 512 + i * 64, 64), :], 0.0))
            his.append(hi)
            los.append(lo)
        parts[i % 2][0].append(jnp.concatenate(his, axis=1))
        parts[i % 2][1].append(jnp.concatenate(los, axis=1))
    return [[jnp.concatenate(p, axis=0) for p in pp] for pp in parts]


def one_hot(first, count, target):
    row = lax.broadcasted_iota(jnp.int32, (count, 128), 0) + first
    return jnp.where(row == target, 1.0, 0.0).astype(BF)


def point_pair(ge, go, q, r0, rows):
    even, odd = {}, {}
    for d in range(3):
        for c in range(3):
            at = (pl.ds(pl.multiple_of(d * 256 + q * 64 + r0, 8), rows), pl.ds(c * 128, 128))
            even[d, c], odd[d, c] = ge[at], go[at]

    def strain(g):
        return [
            g[0, 0], g[1, 1], g[2, 2],
            0.5 * (g[0, 1] + g[1, 0]), 0.5 * (g[0, 2] + g[2, 0]), 0.5 * (g[1, 2] + g[2, 1]),
        ]

    near = {k: even[k] + odd[k] for k in even}
    far = {k: odd[k] - even[k] if k[0] == 0 else even[k] - odd[k] for k in even}
    return strain(near), strain(far)


def contract(a, b):
    return (a[0] * b[0] + a[1] * b[1] + a[2] * b[2]) + 2.0 * (a[3] * b[3] + a[4] * b[4] + a[5] * b[5])


def first_kernel(
    weights, wsum,
    order_ref, u_ref, v_ref, send_ref, par_ref, grad_ref, ztrace_ref, wjk_ref,
    eu_ref, ab_ref, own_ref, tab_ref, visc_ref, s0_ref, s1_ref, s2_ref, s3_ref,
    ge, go, vm,
):
    order = order_ref[...]
    lev = level()
    us = [[], []]
    for i in range(8):
        live = alive(lev, i, order)
        row = [
            jnp.where(live, u_ref[pl.ds(c * 512 + i * 64, 64), :].astype(F32), 0.0).astype(BF)
            for c in range(3)
        ]
        us[i % 2].append(jnp.concatenate(row, axis=1))
    for par, out in ((0, ge), (1, go)):
        u = jnp.concatenate(us[par], axis=0)
        out[...] = dot(grad_ref[par], jnp.concatenate([u, u], axis=0))

    for i in range(8):
        live = alive(lev, i, order)
        for c in range(3):
            at = pl.ds(c * 512 + i * 64, 64)
            vm[at, :] = jnp.where(live, v_ref[at, :], 0.0)

    total = jnp.zeros((8, 128), F32)
    for q in range(4):

        def points(m, acc, q=q):
            r0 = pl.multiple_of(m * 8, 8)
            w = wjk_ref[pl.ds(r0, 8), :] * weights[q]
            for at, e in zip((q, 7 - q), point_pair(ge, go, q, r0, 8)):
                inv = lax.rsqrt(2.0 * contract(e, e) + DELTA * DELTA)
                wmu = w + (2.0 * w) * inv
                acc = acc + wmu
                here = pl.multiple_of(at * 64 + r0, 8)
                for s in range(6):
                    eu_ref[pl.ds(s * 512 + here, 8), :] = e[s]
                ab_ref[pl.ds(here, 8), :] = 2.0 * wmu
                ab_ref[pl.ds(512 + here, 8), :] = (8.0 * w) * (inv * inv * inv)
            return acc

        total = lax.fori_loop(0, 8, points, total, unroll=2)
    visc = jnp.sum(total, axis=0, keepdims=True) * (1.0 / wsum)
    visc_ref[...] = jnp.broadcast_to(visc, (8, 128))

    def put(c, row, rows, d, even_v, odd_v, even_g, odd_g):
        for s in range(2):
            lanes = pl.ds((2 * d + s) * 128, 128)
            t = even_v + odd_v if s else even_v - odd_v
            g = even_g + odd_g if s else even_g - odd_g
            own_ref[pl.ds(c * 64 + row, rows), lanes] = t
            own_ref[pl.ds(192 + c * 64 + row, rows), lanes] = g * visc

    def sums(get):
        v = [get(i) for i in range(8)]
        return (
            (v[0] + v[2]) + (v[4] + v[6]),
            (v[1] + v[3]) + (v[5] + v[7]),
            (3.0 * v[2] + 10.0 * v[4]) + 21.0 * v[6],
            (v[1] + 6.0 * v[3]) + (15.0 * v[5] + 28.0 * v[7]),
        )

    for c in range(3):
        for m in range(8):
            put(c, m * 8, 8, 0, *sums(lambda i: vm[pl.ds(c * 512 + i * 64 + m * 8, 8), :]))
        for i in range(8):
            put(c, i * 8, 8, 1, *sums(lambda j: vm[pl.ds(c * 512 + i * 64 + j * 8, 8), :]))
    pieces = [split(vm[pl.ds(c * 512, 512), :]) for c in range(3)]
    both = jnp.concatenate([jnp.concatenate([p[k] for p in pieces], axis=1) for k in range(2)], axis=0)
    zt = ztrace_ref[...]
    z = dot(jnp.concatenate([zt, zt], axis=1), both)
    for c in range(3):
        for s in range(2):
            lanes = pl.ds((4 + s) * 128, 128)
            block = z[:, c * 128 : (c + 1) * 128]
            own_ref[pl.ds(c * 64, 64), lanes] = block[s * 64 : (s + 1) * 64]
            own_ref[pl.ds(192 + c * 64, 64), lanes] = block[128 + s * 64 : 192 + s * 64] * visc

    for f in range(6):
        lanes = pl.ds(f * 128, 128)
        for r in range(0, 384, 64):
            hi, lo = split(own_ref[pl.ds(r, 64), lanes])
            tab_ref[pl.ds(r, 64), lanes] = hi
            tab_ref[pl.ds(r, 64), pl.ds(768 + f * 128, 128)] = lo
    row = lax.broadcasted_iota(jnp.int32, (16, 128), 0)
    extra = jnp.where(row == 0, visc, jnp.where(row == 1, order.astype(F32), 0.0))
    hi, lo = split(extra)
    for f in range(6):
        tab_ref[pl.ds(384, 16), pl.ds(f * 128, 128)] = hi
        tab_ref[pl.ds(384, 16), pl.ds(768 + f * 128, 128)] = lo

    up_x, up_y = par_ref[0] == 0, par_ref[1] == 0
    rows = [send_ref[k : k + 1, :] for k in range(4)]
    picks = [
        jnp.where(up_y, rows[2], rows[3]),
        jnp.where(up_y, rows[3], rows[2]),
        jnp.where(up_x, rows[0], rows[1]),
        jnp.where(up_x, rows[1], rows[0]),
    ]
    hot = jnp.concatenate([one_hot(0, 768, p) for p in picks], axis=1)
    packet = dot(tab_ref[...], jnp.concatenate([hot, hot], axis=0))
    for k, out in enumerate((s0_ref, s1_ref, s2_ref, s3_ref)):
        out[...] = packet[:392, k * 128 : (k + 1) * 128]


def volume_kernel(
    order_ref, v_ref, eu_ref, ab_ref, grad_ref, div_ref, tab_ref, links_ref,
    vol_ref, far_ref,
    ge, go, sp,
):
    parts = masked_split(v_ref, order_ref[...])
    for par, out in ((0, ge), (1, go)):
        hi, lo = parts[par]
        mat = grad_ref[par]
        left = jnp.concatenate([mat[:, :256], mat], axis=1)
        out[...] = dot(left, jnp.concatenate([hi, lo, hi], axis=0))

    for q in range(4):

        def points(m, carry, q=q):
            r0 = pl.multiple_of(m * 16, 16)
            plus, minus = [[] for _ in range(6)], [[] for _ in range(6)]
            for half in range(2):
                rr = r0 + half * 8
                stress = []
                for at, ev in zip((q, 7 - q), point_pair(ge, go, q, rr, 8)):
                    here = pl.multiple_of(at * 64 + rr, 8)
                    eu = [eu_ref[pl.ds(s * 512 + here, 8), :] for s in range(6)]
                    a = ab_ref[pl.ds(here, 8), :]
                    b = ab_ref[pl.ds(512 + here, 8), :] * contract(eu, ev)
                    stress.append([a * ev[s] - b * eu[s] for s in range(6)])
                for s in range(6):
                    plus[s].append(stress[0][s] + stress[1][s])
                    minus[s].append(stress[0][s] - stress[1][s])
            for s in range(6):
                for k, value in enumerate((plus[s], minus[s])):
                    for j, piece in enumerate(split(jnp.concatenate(value, axis=0))):
                        base = ((s * 2 + k) * 2 + j) * 256 + q * 64
                        sp[pl.ds(pl.multiple_of(base + r0, 16), 16), :] = piece
            return carry

        lax.fori_loop(0, 4, points, 0)

    for par in range(2):
        halves = []
        for j in range(2):
            rows = []
            for d in range(3):
                k = (1 if d == 0 else 0) ^ par
                rows.append(
                    jnp.concatenate(
                        [sp[pl.ds(((SYM[d][c] * 2 + k) * 2 + j) * 256, 256), :] for c in range(3)], axis=1
                    )
                )
            halves.append(jnp.concatenate(rows, axis=0))
        mat = div_ref[par]
        left = jnp.concatenate([mat[:, :768], mat], axis=1)
        out = dot(left, jnp.concatenate([halves[0], halves[1], halves[0]], axis=0))
        for ii in range(4):
            for c in range(3):
                vol_ref[pl.ds(c * 512 + (2 * ii + par) * 64, 64), :] = out[
                    ii * 64 : ii * 64 + 64, c * 128 : c * 128 + 128
                ]

    hot = jnp.concatenate([one_hot(0, 768, links_ref[f : f + 1, :]) for f in range(6)], axis=1)
    far_ref[...] = dot(tab_ref[...], jnp.concatenate([hot, hot], axis=0))


def face_kernel(
    order_ref, far_ref, r0_ref, r1_ref, r2_ref, r3_ref, own_ref, visc_ref, links_ref, orient_ref, par_ref,
    vol_ref, zlift_ref, mab_ref,
    out_ref,
    got, acc, zin,
):
    order = order_ref[...]
    his, los = [], []
    for r in (r0_ref, r1_ref, r2_ref, r3_ref):
        hi, lo = split(jnp.concatenate([r[...], jnp.zeros((8, 128), F32)], axis=0))
        his.append(hi)
        los.append(lo)
    flip_x, flip_y = par_ref[0], par_ref[1]
    hots = []
    for f in range(6):
        link = links_ref[f : f + 1, :]
        slot = link - 768
        k = slot // 128
        block = jnp.where(k < 2, 2 + (k ^ flip_x), (k - 2) ^ flip_y)
        mapped = jnp.where((slot < 0) | (slot >= 512), -1, block * 128 + slot % 128)
        hots.append(one_hot(0, 512, mapped))
    hot = jnp.concatenate(hots, axis=1)
    left = jnp.concatenate(his + los, axis=1)
    got[...] = far_ref[...] + dot(left, jnp.concatenate([hot, hot], axis=0))

    visc = visc_ref[0:1, :]
    odd_b = lax.broadcasted_iota(jnp.int32, (8, 128), 0) % 2 == 1
    orderf = order.astype(F32)
    face = []
    for f in range(6):
        lanes = pl.ds(f * 128, 128)
        bits = orient_ref[f : f + 1, :]
        first = jnp.where(bits % 2 == 1, -1.0, 1.0)
        second = jnp.where(odd_b & (bits >= 2), -1.0, 1.0)
        spin = (second, second * first)
        far_visc, far_order = got[pl.ds(384, 1), lanes], got[pl.ds(385, 1), lanes]
        share = jnp.where(links_ref[f : f + 1, :] == 1280, 1.0, 0.5)
        top = jnp.maximum(orderf, far_order) + 1.0
        penalty = 2.0 * top * top * jnp.maximum(visc, far_visc)
        face.append((lanes, spin, share, penalty, share * visc))

    def flux(f, c, a):
        lanes, spin, share, penalty, weak = face[f]
        row, row_h = pl.ds(c * 64 + a * 8, 8), pl.ds(192 + c * 64 + a * 8, 8)
        rot = spin[a % 2]
        mm = mab_ref[pl.ds(a * 8, 8), :]
        jump = own_ref[row, lanes] - rot * got[row, lanes]
        value = mm * (penalty * jump - share * (own_ref[row_h, lanes] - rot * got[row_h, lanes]))
        return value, mm * (-weak * jump)

    def pair(d, c, a):
        v0, g0 = flux(2 * d, c, a)
        v1, g1 = flux(2 * d + 1, c, a)
        return v1 + v0, v1 - v0, g1 + g0, g1 - g0

    for c in range(3):
        for a in range(8):
            parts = pair(2, c, a)
            for k in range(4):
                zin[pl.ds(k * 64 + a * 8, 8), pl.ds(c * 128, 128)] = parts[k]
    hi, lo = split(zin[...])
    zl = zlift_ref[...]
    acc[...] = dot(jnp.concatenate([zl, zl], axis=1), jnp.concatenate([hi, lo], axis=0))

    lev = level()
    for c in range(3):
        lanes = pl.ds(c * 128, 128)
        for a in range(8):
            ve, vo, ge, go = pair(1, c, a)
            for j in range(8):
                at = pl.ds(a * 64 + j * 8, 8)
                acc[at, lanes] = acc[at, lanes] + ((vo + SLOPE[j] * go) if j % 2 else (ve + SLOPE[j] * ge))
        for a in range(8):
            ve, vo, ge, go = pair(0, c, a)
            for i in range(8):
                at = pl.ds(i * 64 + a * 8, 8)
                to = pl.ds(c * 512 + i * 64 + a * 8, 8)
                value = acc[at, lanes] + ((vo + SLOPE[i] * go) if i % 2 else (ve + SLOPE[i] * ge))
                live = alive(lev[a * 8 : a * 8 + 8], i, order)
                out_ref[to, :] = jnp.where(live, vol_ref[to, :] + value, 0.0)


def shape(rows, cols=128, kind=F32):
    return jax.ShapeDtypeStruct((rows, cols), kind)


VM = pl.BlockSpec(memory_space=pltpu.VMEM)
SM = pl.BlockSpec(memory_space=pltpu.SMEM)


def pairs(count, first):
    return [p for s in range(first, count - 1, 2) for p in ((s, s + 1), (s + 1, s))]


def exchange(value, axis, first):
    return lax.ppermute(value, axis, pairs(lax.axis_size(axis), first))


def body(orders, velocity, adjoint_field, face_links, orient, send_faces):
    tab = tables()
    order = orders[0]
    u = velocity.reshape(1536, 128)
    v = adjoint_field.reshape(1536, 128)
    par = jnp.stack([lax.axis_index("gx") % 2, lax.axis_index("gy") % 2]).astype(jnp.int32)
    grad, div = jnp.asarray(tab["grad"]), jnp.asarray(tab["div"])
    eu, ab, own, table, visc, *packets = pl.pallas_call(
        functools.partial(first_kernel, tab["w"], tab["wsum"]),
        out_shape=[shape(3072), shape(1024), shape(384, 768), shape(400, 1536, BF), shape(8)] + [shape(392)] * 4,
        in_specs=[VM, VM, VM, VM, SM, VM, VM, VM],
        out_specs=[VM] * 9,
        scratch_shapes=[pltpu.VMEM((768, 384), F32), pltpu.VMEM((768, 384), F32), pltpu.VMEM((1536, 128), F32)],
        name="state_and_traces",
    )(order, u, v, send_faces[0, 0], par, grad, jnp.asarray(tab["ztrace"]), jnp.asarray(tab["wjk"]))
    got = [
        exchange(packets[0], "gy", 0),
        exchange(packets[1], "gy", 1),
        exchange(packets[2], "gx", 0),
        exchange(packets[3], "gx", 1),
    ]
    vol, far = pl.pallas_call(
        volume_kernel,
        out_shape=[shape(1536), shape(400, 768)],
        in_specs=[VM] * 8,
        out_specs=[VM] * 2,
        scratch_shapes=[pltpu.VMEM((768, 384), F32), pltpu.VMEM((768, 384), F32), pltpu.VMEM((6144, 128), BF)],
        name="volume",
    )(order, v, eu, ab, grad, div, table, face_links[0, 0])
    out = pl.pallas_call(
        face_kernel,
        out_shape=shape(1536),
        in_specs=[VM] * 10 + [SM] + [VM] * 3,
        out_specs=VM,
        scratch_shapes=[pltpu.VMEM((400, 768), F32), pltpu.VMEM((512, 384), F32), pltpu.VMEM((256, 384), F32)],
        name="faces",
    )(
        order, far, *got, own, visc, face_links[0, 0], orient[0, 0], par, vol,
        jnp.asarray(tab["zlift"]), jnp.asarray(tab["mab"]),
    )
    return out.reshape(1, 1, 3, 512, 128)


def solution(mesh):
    return jax.shard_map(
        body,
        mesh=mesh,
        in_specs=(
            P("gx", "gy", None),
            P("gx", "gy", None, None, None),
            P("gx", "gy", None, None, None),
            P("gx", "gy", None, None),
            P("gx", "gy", None, None),
            P("gx", "gy", None, None),
        ),
        out_specs=P("gx", "gy", None, None, None),
        check_vma=False,
    )
```

profile of v0, /device:TPU:12, one launch (start us, length us, event | category | flops | bytes accessed | tf_op | source)
XLA Modules:
  0.0 31.2 jit_solution(9181200925239763612)
XLA Ops:
  0.0 0.0 copy-start.4
  0.0 0.0 copy-start.5
  0.0 0.6 %pad_add_fusion.par_ref = s32[2]{0:T(128)} fusion(s32[1]{0:T(128)} %bitcast.5, s32[1]{0:T(128)} %bitcast.4), kind=kLoop, calls=%fused_computation.2 | loop fusion | flops 2 | bytes 16 | tf_op jit(solution)/shard_map/stack | solution.py:403
  0.6 6.1 %state_and_traces.1 = (f32[3072,128]{1,0:T(8,128)}, f32[1024,128]{1,0:T(8,128)}, f32[384,768]{1,0:T(8,128)}, bf16[400,1536]{1,0:T(8,128)(2,1)}, f32[8,128]{1,0:T...) custom-call(s32[1,128]{1,0:T(1,128)} %bitcast.14, ...), custom_call_target="tpu_custom_call" | custom-call | tf_op jit(solution)/shard_map/state_and_traces/pallas_call | solution.py:405
  6.7 0.0 collective-permute-start
  6.7 3.4 %collective-permute-start.1 = (f32[392,128]{1,0:T(8,128)}, f32[392,128]{1,0:T(8,128)S(1)}, u32[]{:S(2)}, u32[]{:S(2)}) collective-permute-start(f32[392,128]{1,0:T(8,128)} %get-tuple-element.21), channel_id=1, source_target_pairs={{1,2},{2,1},{3,4},{4,3},{5,6},{6,5},{9,10},{10,9},{11,12},{12,11},... | collective-permute-start | bytes 602120 | tf_op jit(solution)/shard_map/ppermute | solution.py:395
  10.1 0.5 %collective-permute-start.2 = (f32[392,128]{1,0:T(8,128)}, f32[392,128]{1,0:T(8,128)S(1)}, u32[]{:S(2)}, u32[]{:S(2)}) collective-permute-start(f32[392,128]{1,0:T(8,128)} %get-tuple-element.22), channel_id=1, source_target_pairs={{0,8},{8,0},{16,24},{24,16},{1,9},{9,1},{17,25},{25,17},{2,10},{10... | collective-permute-start | bytes 602120 | tf_op jit(solution)/shard_map/ppermute | solution.py:395
  10.7 4.6 %collective-permute-start.3 = (f32[392,128]{1,0:T(8,128)}, f32[392,128]{1,0:T(8,128)S(1)}, u32[]{:S(2)}, u32[]{:S(2)}) collective-permute-start(f32[392,128]{1,0:T(8,128)} %get-tuple-element.23), channel_id=1, source_target_pairs={{8,16},{16,8},{9,17},{17,9},{10,18},{18,10},{11,19},{19,11},{12,20... | collective-permute-start | bytes 602120 | tf_op jit(solution)/shard_map/ppermute | solution.py:395
  15.3 0.0 copy-done.4
  15.3 0.0 copy-done.5
  15.3 0.6 %copy_bitcast_fusion = (s32[6,128]{1,0:T(8,128)}, s32[6,128]{1,0:T(8,128)}) fusion(s32[1,1,6,128]{3,1,2,0:T(1,128)S(1)} %copy-done.4, s32[1,1,6,128]{3,1,2,0:T(1,128)S(1)} %copy-done.5), kind=kLoop, calls=%fused_computation | loop fusion | bytes 12288
  15.9 9.5 %volume.1 = (f32[1536,128]{1,0:T(8,128)}, f32[400,768]{1,0:T(8,128)}) custom-call(s32[1,128]{1,0:T(1,128)} %bitcast.15, f32[1536,128]{1,0:T(8,128)} %bitcast.12, f32[3072,128]{1,0:T(8,128)} %get-tuple-element.16.eu_ref, f32[1024,128]{1,0:T(8,128)} %get-tuple-element.17.ab_ref, bf16[2,768,512]{2,1,0:T(8,128)(2,1)} %constant.37.clone.grad_ref, ...), custom_call_target="tpu_custom_call" | custom-call | tf_op jit(solution)/shard_map/volume/pallas_call | solution.py:419
  25.4 0.0 collective-permute-done.r0_ref
  25.4 0.0 copy-start
  25.4 0.0 collective-permute-done.1.r1_ref
  25.4 0.0 copy-start.1
  25.4 0.0 collective-permute-done.2.r2_ref
  25.4 0.0 copy-start.2
  25.4 0.0 collective-permute-done.3.r3_ref
  25.4 0.0 copy-start.3
  25.4 0.6 %copy-done = f32[392,128]{1,0:T(8,128)} copy-done((f32[392,128]{1,0:T(8,128)}, f32[392,128]{1,0:T(8,128)S(1)}, u32[]{:S(2)}) %copy-start) | copy-done | bytes 200728
  26.1 0.1 copy-done.1
  26.1 0.1 copy-done.2
  26.2 0.1 copy-done.3
  26.3 5.0 %faces.1 = f32[1536,128]{1,0:T(8,128)} custom-call(s32[1,128]{1,0:T(1,128)} %bitcast.16, f32[400,768]{1,0:T(8,128)} %get-tuple-element.19.far_ref, f32[392,128]{1,0:T(8,128)} %copy-done, f32[392,128]{1,0:T(8,128)} %copy-done.1, f32[392,128]{1,0:T(8,128)} %copy-done.2, f32[392,128]{1,0:T(8,128)} %copy-done.3, f32[384,768]{1,0:T(8,128)} %get-tuple-element.24.own_ref, ...), custom_call_target="tpu_custom_call" | custom-call | tf_op jit(solution)/shard_map/faces/pallas_call | solution.py:427
Async XLA Ops:
  0.0 15.3 %copy-start.4 = (s32[1,1,6,128]{3,1,2,0:T(1,128)S(1)}, s32[1,1,6,128]{3,1,2,0:T(1,128)}, u32[]{:S(2)}) copy-start(s32[1,1,6,128]{3,1,2,0:T(1,128)} %param.16) | copy-start | bytes 9220
  0.0 15.3 %copy-start.5 = (s32[1,1,6,128]{3,1,2,0:T(1,128)S(1)}, s32[1,1,6,128]{3,1,2,0:T(1,128)}, u32[]{:S(2)}) copy-start(s32[1,1,6,128]{3,1,2,0:T(1,128)} %param.15) | copy-start | bytes 9220
  6.7 18.7 %collective-permute-start = (f32[392,128]{1,0:T(8,128)}, f32[392,128]{1,0:T(8,128)S(1)}, u32[]{:S(2)}, u32[]{:S(2)}) collective-permute-start(f32[392,128]{1,0:T(8,128)} %get-tuple-element.20), channel_id=1, source_target_pairs={{0,1},{1,0},{2,3},{3,2},{4,5},{5,4},{6,7},{7,6},{8,9},{9,8},{10,11... | collective-permute-start | bytes 602120 | tf_op jit(solution)/shard_map/ppermute | solution.py:395
  6.7 18.7 %collective-permute-start.1 = (f32[392,128]{1,0:T(8,128)}, f32[392,128]{1,0:T(8,128)S(1)}, u32[]{:S(2)}, u32[]{:S(2)}) collective-permute-start(f32[392,128]{1,0:T(8,128)} %get-tuple-element.21), channel_id=1, source_target_pairs={{1,2},{2,1},{3,4},{4,3},{5,6},{6,5},{9,10},{10,9},{11,12},{12,11},... | collective-permute-start | bytes 602120 | tf_op jit(solution)/shard_map/ppermute | solution.py:395
  10.1 15.2 %collective-permute-start.2 = (f32[392,128]{1,0:T(8,128)}, f32[392,128]{1,0:T(8,128)S(1)}, u32[]{:S(2)}, u32[]{:S(2)}) collective-permute-start(f32[392,128]{1,0:T(8,128)} %get-tuple-element.22), channel_id=1, source_target_pairs={{0,8},{8,0},{16,24},{24,16},{1,9},{9,1},{17,25},{25,17},{2,10},{10... | collective-permute-start | bytes 602120 | tf_op jit(solution)/shard_map/ppermute | solution.py:395
  10.7 14.7 %collective-permute-start.3 = (f32[392,128]{1,0:T(8,128)}, f32[392,128]{1,0:T(8,128)S(1)}, u32[]{:S(2)}, u32[]{:S(2)}) collective-permute-start(f32[392,128]{1,0:T(8,128)} %get-tuple-element.23), channel_id=1, source_target_pairs={{8,16},{16,8},{9,17},{17,9},{10,18},{18,10},{11,19},{19,11},{12,20... | collective-permute-start | bytes 602120 | tf_op jit(solution)/shard_map/ppermute | solution.py:395
  25.4 0.7 %copy-start = (f32[392,128]{1,0:T(8,128)}, f32[392,128]{1,0:T(8,128)S(1)}, u32[]{:S(2)}) copy-start(f32[392,128]{1,0:T(8,128)S(1)} %collective-permute-done.r0_ref) | copy-start | bytes 602116
  25.4 0.7 %copy-start.1 = (f32[392,128]{1,0:T(8,128)}, f32[392,128]{1,0:T(8,128)S(1)}, u32[]{:S(2)}) copy-start(f32[392,128]{1,0:T(8,128)S(1)} %collective-permute-done.1.r1_ref) | copy-start | bytes 602116
  25.4 0.8 %copy-start.2 = (f32[392,128]{1,0:T(8,128)}, f32[392,128]{1,0:T(8,128)S(1)}, u32[]{:S(2)}) copy-start(f32[392,128]{1,0:T(8,128)S(1)} %collective-permute-done.2.r2_ref) | copy-start | bytes 602116
  25.4 0.9 %copy-start.3 = (f32[392,128]{1,0:T(8,128)}, f32[392,128]{1,0:T(8,128)S(1)}, u32[]{:S(2)}) copy-start(f32[392,128]{1,0:T(8,128)S(1)} %collective-permute-done.3.r3_ref) | copy-start | bytes 602116
where the time goes:
time: 31.4 us; the launch traced here: 31.2 us
  Pallas kernels  20.5 us (65%)
  starting transfers between devices  8.56 us (27%)
  local copies, waits for them, and re-layouts  1.46 us (5%)
  other arithmetic  0.59 us (2%)
    pallas_call x1, Pallas kernels, body(): pl.pallas_call(volume_kernel, out_shape=[shape(1536), shape(400, 768)], i...  9.47 us
    ppermute x4, starting transfers between devices, exchange(): return lax.ppermute(value, axis, pairs(lax.axis_size(axis), first))  8.56 us
    pallas_call x1, Pallas kernels, body(): pl.pallas_call(functools.partial(first_kernel, tab['w'], tab['wsum']), ou...  6.1 us
    pallas_call x1, Pallas kernels, body(): pl.pallas_call(face_kernel, out_shape=shape(1536), in_specs=[VM] * 10 + [...  4.97 us
    unnamed x13, local copies, waits for them, and re-layouts  1.46 us
  transfers between devices with their start and end apart: 4, of which 0 were waited for; matrix products, arithmetic and copies ran while one was open for 2% of the time, Pallas kernels for 30%

commit v1 on v0

--- a/solution.py
+++ b/solution.py
@@ -85,21 +85,6 @@
     return jnp.maximum(lev, i) <= order
 
 
-def masked_split(v_ref, order):
-    lev = level()
-    parts = [[[], []], [[], []]]
-    for i in range(8):
-        live = alive(lev, i, order)
-        his, los = [], []
-        for c in range(3):
-            hi, lo = split(jnp.where(live, v_ref[pl.ds(c * 512 + i * 64, 64), :], 0.0))
-            his.append(hi)
-            los.append(lo)
-        parts[i % 2][0].append(jnp.concatenate(his, axis=1))
-        parts[i % 2][1].append(jnp.concatenate(los, axis=1))
-    return [[jnp.concatenate(p, axis=0) for p in pp] for pp in parts]
-
-
 def one_hot(first, count, target):
     row = lax.broadcasted_iota(jnp.int32, (count, 128), 0) + first
     return jnp.where(row == target, 1.0, 0.0).astype(BF)
@@ -129,10 +114,20 @@
 
 def first_kernel(
     weights, wsum,
-    order_ref, u_ref, v_ref, send_ref, par_ref, grad_ref, ztrace_ref, wjk_ref,
-    eu_ref, ab_ref, own_ref, tab_ref, visc_ref, s0_ref, s1_ref, s2_ref, s3_ref,
-    ge, go, vm,
+    order_hbm, u_hbm, v_hbm, send_hbm, grad_hbm, ztrace_hbm, wjk_hbm,
+    eu_ref, ab_ref, own_ref, tab_ref, visc_ref, vhi_ref, vlo_ref, s0_ref, s1_ref, s2_ref, s3_ref,
+    order_ref, u_ref, v_ref, send_ref, grad_ref, ztrace_ref, wjk_ref, ge, go, vm, sems,
 ):
+    names = ("order", "u", "grad", "v", "wjk", "ztrace", "send")
+    ends = (
+        (order_hbm, order_ref), (u_hbm, u_ref), (grad_hbm, grad_ref), (v_hbm, v_ref),
+        (wjk_hbm, wjk_ref), (ztrace_hbm, ztrace_ref), (send_hbm, send_ref),
+    )
+    loads = {n: pltpu.make_async_copy(*e, sems.at[k]) for k, (n, e) in enumerate(zip(names, ends))}
+    for n in names:
+        loads[n].start()
+    loads["order"].wait()
+    loads["u"].wait()
     order = order_ref[...]
     lev = level()
     us = [[], []]
@@ -143,15 +138,22 @@
             for c in range(3)
         ]
         us[i % 2].append(jnp.concatenate(row, axis=1))
+    loads["grad"].wait()
     for par, out in ((0, ge), (1, go)):
         u = jnp.concatenate(us[par], axis=0)
         out[...] = dot(grad_ref[par], jnp.concatenate([u, u], axis=0))
 
+    loads["v"].wait()
+    loads["wjk"].wait()
+    loads["ztrace"].wait()
+    loads["send"].wait()
     for i in range(8):
         live = alive(lev, i, order)
         for c in range(3):
             at = pl.ds(c * 512 + i * 64, 64)
-            vm[at, :] = jnp.where(live, v_ref[at, :], 0.0)
+            value = jnp.where(live, v_ref[at, :], 0.0)
+            vm[at, :] = value
+            vhi_ref[at, :], vlo_ref[at, :] = split(value)
 
     total = jnp.zeros((8, 128), F32)
     for q in range(4):
@@ -196,8 +198,9 @@
             put(c, m * 8, 8, 0, *sums(lambda i: vm[pl.ds(c * 512 + i * 64 + m * 8, 8), :]))
         for i in range(8):
             put(c, i * 8, 8, 1, *sums(lambda j: vm[pl.ds(c * 512 + i * 64 + j * 8, 8), :]))
-    pieces = [split(vm[pl.ds(c * 512, 512), :]) for c in range(3)]
-    both = jnp.concatenate([jnp.concatenate([p[k] for p in pieces], axis=1) for k in range(2)], axis=0)
+    both = jnp.concatenate(
+        [jnp.concatenate([r[pl.ds(c * 512, 512), :] for c in range(3)], axis=1) for r in (vhi_ref, vlo_ref)], axis=0
+    )
     zt = ztrace_ref[...]
     z = dot(jnp.concatenate([zt, zt], axis=1), both)
     for c in range(3):
@@ -220,8 +223,8 @@
         tab_ref[pl.ds(384, 16), pl.ds(f * 128, 128)] = hi
         tab_ref[pl.ds(384, 16), pl.ds(768 + f * 128, 128)] = lo
 
-    up_x, up_y = par_ref[0] == 0, par_ref[1] == 0
-    rows = [send_ref[k : k + 1, :] for k in range(4)]
+    up_x, up_y = lax.axis_index("gx") % 2 == 0, lax.axis_index("gy") % 2 == 0
+    rows = [send_ref[0, 0, k : k + 1, :] for k in range(4)]
     picks = [
         jnp.where(up_y, rows[2], rows[3]),
         jnp.where(up_y, rows[3], rows[2]),
@@ -235,13 +238,23 @@
 
 
 def volume_kernel(
-    order_ref, v_ref, eu_ref, ab_ref, grad_ref, div_ref, tab_ref, links_ref,
+    vhi_ref, vlo_ref, eu_ref, ab_ref, grad_ref, div_hbm, tab_ref, links_ref,
     vol_ref, far_ref,
-    ge, go, sp,
+    div_ref, ge, go, sp, sem,
 ):
-    parts = masked_split(v_ref, order_ref[...])
+    load = pltpu.make_async_copy(div_hbm, div_ref, sem)
+    load.start()
     for par, out in ((0, ge), (1, go)):
-        hi, lo = parts[par]
+        hi, lo = (
+            jnp.concatenate(
+                [
+                    jnp.concatenate([r[pl.ds(c * 512 + i * 64, 64), :] for c in range(3)], axis=1)
+                    for i in range(par, 8, 2)
+                ],
+                axis=0,
+            )
+            for r in (vhi_ref, vlo_ref)
+        )
         mat = grad_ref[par]
         left = jnp.concatenate([mat[:, :256], mat], axis=1)
         out[...] = dot(left, jnp.concatenate([hi, lo, hi], axis=0))
@@ -272,6 +285,7 @@
 
         lax.fori_loop(0, 4, points, 0)
 
+    load.wait()
     for par in range(2):
         halves = []
         for j in range(2):
@@ -293,12 +307,12 @@
                     ii * 64 : ii * 64 + 64, c * 128 : c * 128 + 128
                 ]
 
-    hot = jnp.concatenate([one_hot(0, 768, links_ref[f : f + 1, :]) for f in range(6)], axis=1)
+    hot = jnp.concatenate([one_hot(0, 768, links_ref[f]) for f in range(6)], axis=1)
     far_ref[...] = dot(tab_ref[...], jnp.concatenate([hot, hot], axis=0))
 
 
 def face_kernel(
-    order_ref, far_ref, r0_ref, r1_ref, r2_ref, r3_ref, own_ref, visc_ref, links_ref, orient_ref, par_ref,
+    order_ref, far_ref, r0_ref, r1_ref, r2_ref, r3_ref, own_ref, visc_ref, links_ref, orient_ref,
     vol_ref, zlift_ref, mab_ref,
     out_ref,
     got, acc, zin,
@@ -309,10 +323,10 @@
         hi, lo = split(jnp.concatenate([r[...], jnp.zeros((8, 128), F32)], axis=0))
         his.append(hi)
         los.append(lo)
-    flip_x, flip_y = par_ref[0], par_ref[1]
+    flip_x, flip_y = lax.axis_index("gx") % 2, lax.axis_index("gy") % 2
     hots = []
     for f in range(6):
-        link = links_ref[f : f + 1, :]
+        link = links_ref[f]
         slot = link - 768
         k = slot // 128
         block = jnp.where(k < 2, 2 + (k ^ flip_x), (k - 2) ^ flip_y)
@@ -328,12 +342,12 @@
     face = []
     for f in range(6):
         lanes = pl.ds(f * 128, 128)
-        bits = orient_ref[f : f + 1, :]
+        bits = orient_ref[f]
         first = jnp.where(bits % 2 == 1, -1.0, 1.0)
         second = jnp.where(odd_b & (bits >= 2), -1.0, 1.0)
         spin = (second, second * first)
         far_visc, far_order = got[pl.ds(384, 1), lanes], got[pl.ds(385, 1), lanes]
-        share = jnp.where(links_ref[f : f + 1, :] == 1280, 1.0, 0.5)
+        share = jnp.where(links_ref[f] == 1280, 1.0, 0.5)
         top = jnp.maximum(orderf, far_order) + 1.0
         penalty = 2.0 * top * top * jnp.maximum(visc, far_visc)
         face.append((lanes, spin, share, penalty, share * visc))
@@ -384,15 +398,35 @@
 
 
 VM = pl.BlockSpec(memory_space=pltpu.VMEM)
-SM = pl.BlockSpec(memory_space=pltpu.SMEM)
-
-
-def pairs(count, first):
-    return [p for s in range(first, count - 1, 2) for p in ((s, s + 1), (s + 1, s))]
+HBM = pl.BlockSpec(memory_space=pltpu.HBM)
+PARAMS = pltpu.CompilerParams(vmem_limit_bytes=20 * 1024 * 1024)
+
+
+def partner(s, count, first):
+    t = s + 1 if (s - first) % 2 == 0 else s - 1
+    return t if first <= min(s, t) and max(s, t) < count else None
 
 
 def exchange(value, axis, first):
-    return lax.ppermute(value, axis, pairs(lax.axis_size(axis), first))
+    gx, gy = lax.axis_size("gx"), lax.axis_size("gy")
+    links = []
+    for x in range(gx):
+        for y in range(gy):
+            if axis == "gx":
+                tx, ty = partner(x, gx, first), y
+                if tx is None:
+                    tx, ty = x, partner(y, gy, 0)
+                    ty = y if ty is None else ty
+            else:
+                tx, ty = x, partner(y, gy, first)
+                if ty is None:
+                    ty = gy - 1 - y if gy % 2 == 0 else y
+            links.append((x * gy + y, tx * gy + ty))
+    return lax.ppermute(value, ("gx", "gy"), links)
+
+
+def in_hbm(x):
+    return pltpu.with_memory_space_constraint(x, pltpu.HBM)
 
 
 def body(orders, velocity, adjoint_field, face_links, orient, send_faces):
@@ -400,16 +434,31 @@
     order = orders[0]
     u = velocity.reshape(1536, 128)
     v = adjoint_field.reshape(1536, 128)
-    par = jnp.stack([lax.axis_index("gx") % 2, lax.axis_index("gy") % 2]).astype(jnp.int32)
     grad, div = jnp.asarray(tab["grad"]), jnp.asarray(tab["div"])
-    eu, ab, own, table, visc, *packets = pl.pallas_call(
+    links, turns = face_links.reshape(6, 1, 128), orient.reshape(6, 1, 128)
+    eu, ab, own, table, visc, vhi, vlo, *packets = pl.pallas_call(
         functools.partial(first_kernel, tab["w"], tab["wsum"]),
-        out_shape=[shape(3072), shape(1024), shape(384, 768), shape(400, 1536, BF), shape(8)] + [shape(392)] * 4,
-        in_specs=[VM, VM, VM, VM, SM, VM, VM, VM],
-        out_specs=[VM] * 9,
-        scratch_shapes=[pltpu.VMEM((768, 384), F32), pltpu.VMEM((768, 384), F32), pltpu.VMEM((1536, 128), F32)],
+        out_shape=[shape(3072), shape(1024), shape(384, 768), shape(400, 1536, BF), shape(8)]
+        + [shape(1536, 128, BF)] * 2
+        + [shape(392)] * 4,
+        in_specs=[HBM] * 7,
+        out_specs=[VM] * 11,
+        scratch_shapes=[
+            pltpu.VMEM((1, 128), jnp.int32),
+            pltpu.VMEM((1536, 128), BF),
+            pltpu.VMEM((1536, 128), F32),
+            pltpu.VMEM((1, 1, 4, 128), jnp.int32),
+            pltpu.VMEM((2, 768, 512), BF),
+            pltpu.VMEM((256, 512), BF),
+            pltpu.VMEM((64, 128), F32),
+            pltpu.VMEM((768, 384), F32),
+            pltpu.VMEM((768, 384), F32),
+            pltpu.VMEM((1536, 128), F32),
+            pltpu.SemaphoreType.DMA((7,)),
+        ],
+        compiler_params=PARAMS,
         name="state_and_traces",
-    )(order, u, v, send_faces[0, 0], par, grad, jnp.asarray(tab["ztrace"]), jnp.asarray(tab["wjk"]))
+    )(*map(in_hbm, (order, u, v, send_faces, grad, jnp.asarray(tab["ztrace"]), jnp.asarray(tab["wjk"]))))
     got = [
         exchange(packets[0], "gy", 0),
         exchange(packets[1], "gy", 1),
@@ -419,20 +468,22 @@
     vol, far = pl.pallas_call(
         volume_kernel,
         out_shape=[shape(1536), shape(400, 768)],
-        in_specs=[VM] * 8,
+        in_specs=[VM] * 5 + [HBM] + [VM] * 2,
         out_specs=[VM] * 2,
-        scratch_shapes=[pltpu.VMEM((768, 384), F32), pltpu.VMEM((768, 384), F32), pltpu.VMEM((6144, 128), BF)],
+        scratch_shapes=[pltpu.VMEM((2, 256, 1536), BF), pltpu.VMEM((768, 384), F32), pltpu.VMEM((768, 384), F32), pltpu.VMEM((6144, 128), BF), pltpu.SemaphoreType.DMA],
+        compiler_params=PARAMS,
         name="volume",
-    )(order, v, eu, ab, grad, div, table, face_links[0, 0])
+    )(vhi, vlo, eu, ab, grad, in_hbm(div), table, links)
     out = pl.pallas_call(
         face_kernel,
         out_shape=shape(1536),
-        in_specs=[VM] * 10 + [SM] + [VM] * 3,
+        in_specs=[VM] * 13,
         out_specs=VM,
         scratch_shapes=[pltpu.VMEM((400, 768), F32), pltpu.VMEM((512, 384), F32), pltpu.VMEM((256, 384), F32)],
+        compiler_params=PARAMS,
         name="faces",
     )(
-        order, far, *got, own, visc, face_links[0, 0], orient[0, 0], par, vol,
+        order, far, *got, own, visc, links, turns, vol,
         jnp.asarray(tab["zlift"]), jnp.asarray(tab["mab"]),
     )
     return out.reshape(1, 1, 3, 512, 128)

time: 31.4 us -> 19.4 us (0.62)
  the two profiles are of different devices: /device:TPU:12 before, /device:TPU:0 now
where the time goes in v1:
time: 19.4 us; the launch traced here: 19.2 us
  Pallas kernels  13.3 us (69%)
  starting transfers between devices  5.68 us (29%)
    pallas_call x1, Pallas kernels, body(): pl.pallas_call(volume_kernel, out_shape=[shape(1536), shape(400, 768)], i...  5.73 us
    ppermute x4, starting transfers between devices, exchange(): return lax.ppermute(value, ('gx', 'gy'), links)  5.68 us
    pallas_call x1, Pallas kernels, body(): pl.pallas_call(functools.partial(first_kernel, tab['w'], tab['wsum']), ou...  4.75 us
    pallas_call x1, Pallas kernels, body(): pl.pallas_call(face_kernel, out_shape=shape(1536), in_specs=[VM] * 13, ou...  2.85 us
  transfers between devices with their start and end apart: 4, of which 0 were waited for; matrix products, arithmetic and copies ran while one was open for 0% of the time, Pallas kernels for 30%

profile of v1, /device:TPU:0, one launch (start us, length us, event | category | flops | bytes accessed | tf_op | source)
XLA Modules:
  0.0 19.2 jit_solution(1740356122430531106)
XLA Ops:
  0.0 0.0 copy-start
  0.0 0.0 copy-start.3
  0.0 4.7 %state_and_traces.1 = (f32[3072,128]{1,0:T(8,128)S(1)}, f32[1024,128]{1,0:T(8,128)S(1)}, f32[384,768]{1,0:T(8,128)S(1)}, bf16[400,1536]{1,0:T(8,128)(2,1)S(1)}, ...) custom-call(s32[1,128]{1,0:T(1,128)} %bitcast.9, ...), custom_call_target="tpu_custom_call" | custom-call | tf_op jit(solution)/shard_map/state_and_traces/pallas_call | solution.py:439
  4.8 0.6 %collective-permute-start = (f32[392,128]{1,0:T(8,128)S(1)}, f32[392,128]{1,0:T(8,128)S(1)}, u32[]{:S(2)}, u32[]{:S(2)}) collective-permute-start(f32[392,128]{1,0:T(8,128)S(1)} %get-tuple-element.24), channel_id=1, source_target_pairs={{0,1},{1,0},{2,3},{3,2},{4,5},{5,4},{6,7},{7,6},{8,9},{9,8},{10,11... | collective-permute-start | bytes 602120 | tf_op jit(solution)/shard_map/ppermute | solution.py:425
  5.3 3.5 %collective-permute-start.1 = (f32[392,128]{1,0:T(8,128)S(1)}, f32[392,128]{1,0:T(8,128)S(1)}, u32[]{:S(2)}, u32[]{:S(2)}) collective-permute-start(f32[392,128]{1,0:T(8,128)S(1)} %get-tuple-element.25), channel_id=1, source_target_pairs={{0,7},{1,2},{2,1},{3,4},{4,3},{5,6},{6,5},{7,0},{8,15},{9,10},{10,... | collective-permute-start | bytes 602120 | tf_op jit(solution)/shard_map/ppermute | solution.py:425
  8.9 1.6 %collective-permute-start.2 = (f32[392,128]{1,0:T(8,128)S(1)}, f32[392,128]{1,0:T(8,128)S(1)}, u32[]{:S(2)}, u32[]{:S(2)}) collective-permute-start(f32[392,128]{1,0:T(8,128)S(1)} %get-tuple-element.26), channel_id=1, source_target_pairs={{0,8},{1,9},{2,10},{3,11},{4,12},{5,13},{6,14},{7,15},{8,0},{9,1},... | collective-permute-start | bytes 602120 | tf_op jit(solution)/shard_map/ppermute | solution.py:425
  10.4 0.0 collective-permute-start.3
  10.4 0.0 copy-done
  10.4 0.0 copy-done.3
  10.4 0.0 copy-start.1
  10.5 0.0 copy-start.2
  10.5 0.0 copy-start.4
  10.5 0.0 copy-start.5
  10.5 5.7 %volume.1 = (f32[1536,128]{1,0:T(8,128)S(1)}, f32[400,768]{1,0:T(8,128)S(1)}) custom-call(bf16[1536,128]{1,0:T(8,128)(2,1)S(1)} %get-tuple-element.18.vhi_ref, bf16[1536,128]{1,0:T(8,128)(2,1)S(1)} %get-tuple-element.19.vlo_ref, f32[3072,128]{1,0:T(8,128)S(1)} %get-tuple-element.20.eu_ref, f32[1024,128]{1,0:T(8,128)S(1)} %get-tuple-element.21.ab_ref, ...), custom_call_target="tpu_custom_call" | custom-call | tf_op jit(solution)/shard_map/volume/pallas_call | solution.py:468
  16.2 0.0 collective-permute-done.r0_ref
  16.2 0.0 collective-permute-done.1.r1_ref
  16.3 0.0 collective-permute-done.2.r2_ref
  16.3 0.0 collective-permute-done.3.r3_ref
  16.3 0.0 copy-done.1
  16.3 0.0 copy-done.2
  16.3 0.0 copy-done.4
  16.3 0.0 copy-done.5
  16.3 2.9 %faces.1 = f32[1536,128]{1,0:T(8,128)} custom-call(s32[1,128]{1,0:T(1,128)S(1)} %bitcast.10, f32[400,768]{1,0:T(8,128)S(1)} %get-tuple-element.23.far_ref, f32[392,128]{1,0:T(8,128)S(1)} %collective-permute-done.r0_ref, f32[392,128]{1,0:T(8,128)S(1)} %collective-permute-done.1.r1_ref, f32[392,128]{1,0:T(8,128)S(1)} %collective-permute-done.2.r2_ref, ...), custom_call_target="tpu_custom_call" | custom-call | tf_op jit(solution)/shard_map/faces/pallas_call | solution.py:477
Async XLA Ops:
  0.0 10.4 %copy-start = (bf16[2,768,512]{2,1,0:T(8,128)(2,1)S(1)}, bf16[2,768,512]{2,1,0:T(8,128)(2,1)}, u32[]{:S(2)}) copy-start(bf16[2,768,512]{2,1,0:T(8,128)(2,1)} %constant.12.clone.grad_hbm.grad_ref) | copy-start | bytes 4718596
  0.0 10.4 %copy-start.3 = (s32[1,1,6,128]{3,1,2,0:T(1,128)S(1)}, s32[1,1,6,128]{3,1,2,0:T(1,128)}, u32[]{:S(2)}) copy-start(s32[1,1,6,128]{3,1,2,0:T(1,128)} %param.15) | copy-start | bytes 9220
  4.8 11.5 %collective-permute-start = (f32[392,128]{1,0:T(8,128)S(1)}, f32[392,128]{1,0:T(8,128)S(1)}, u32[]{:S(2)}, u32[]{:S(2)}) collective-permute-start(f32[392,128]{1,0:T(8,128)S(1)} %get-tuple-element.24), channel_id=1, source_target_pairs={{0,1},{1,0},{2,3},{3,2},{4,5},{5,4},{6,7},{7,6},{8,9},{9,8},{10,11... | collective-permute-start | bytes 602120 | tf_op jit(solution)/shard_map/ppermute | solution.py:425
  5.3 10.9 %collective-permute-start.1 = (f32[392,128]{1,0:T(8,128)S(1)}, f32[392,128]{1,0:T(8,128)S(1)}, u32[]{:S(2)}, u32[]{:S(2)}) collective-permute-start(f32[392,128]{1,0:T(8,128)S(1)} %get-tuple-element.25), channel_id=1, source_target_pairs={{0,7},{1,2},{2,1},{3,4},{4,3},{5,6},{6,5},{7,0},{8,15},{9,10},{10,... | collective-permute-start | bytes 602120 | tf_op jit(solution)/shard_map/ppermute | solution.py:425
  8.9 7.4 %collective-permute-start.2 = (f32[392,128]{1,0:T(8,128)S(1)}, f32[392,128]{1,0:T(8,128)S(1)}, u32[]{:S(2)}, u32[]{:S(2)}) collective-permute-start(f32[392,128]{1,0:T(8,128)S(1)} %get-tuple-element.26), channel_id=1, source_target_pairs={{0,8},{1,9},{2,10},{3,11},{4,12},{5,13},{6,14},{7,15},{8,0},{9,1},... | collective-permute-start | bytes 602120 | tf_op jit(solution)/shard_map/ppermute | solution.py:425
  10.4 5.8 %collective-permute-start.3 = (f32[392,128]{1,0:T(8,128)S(1)}, f32[392,128]{1,0:T(8,128)S(1)}, u32[]{:S(2)}, u32[]{:S(2)}) collective-permute-start(f32[392,128]{1,0:T(8,128)S(1)} %get-tuple-element.27), channel_id=1, source_target_pairs={{0,1},{1,0},{2,3},{3,2},{4,5},{5,4},{6,7},{7,6},{8,16},{9,17},{10,... | collective-permute-start | bytes 602120 | tf_op jit(solution)/shard_map/ppermute | solution.py:425
  10.4 5.8 %copy-start.1 = (bf16[512,256]{1,0:T(8,128)(2,1)S(1)}, bf16[512,256]{1,0:T(8,128)(2,1)}, u32[]{:S(2)}) copy-start(bf16[512,256]{1,0:T(8,128)(2,1)} %constant.16.clone.zlift_ref) | copy-start | bytes 786436
  10.5 5.8 %copy-start.2 = (f32[64,128]{1,0:T(8,128)S(1)}, f32[64,128]{1,0:T(8,128)}, u32[]{:S(2)}) copy-start(f32[64,128]{1,0:T(8,128)} %constant.17.clone.mab_ref) | copy-start | bytes 98308
  10.5 5.8 %copy-start.4 = (s32[1,1,6,128]{3,1,2,0:T(1,128)S(1)}, s32[1,1,6,128]{3,1,2,0:T(1,128)}, u32[]{:S(2)}) copy-start(s32[1,1,6,128]{3,1,2,0:T(1,128)} %param.16) | copy-start | bytes 9220
  10.5 5.8 %copy-start.5 = (s32[1,1,128]{2,1,0:T(1,128)S(1)}, s32[1,1,128]{2,1,0:T(1,128)}, u32[]{:S(2)}) copy-start(s32[1,1,128]{2,1,0:T(1,128)} %param.12) | copy-start | bytes 1540

commit v2 on v1

--- a/solution.py
+++ b/solution.py
@@ -11,6 +11,7 @@
 DELTA = 0.05
 BF = jnp.bfloat16
 F32 = jnp.float32
+MXU_ROWS = 256
 SLOPE = [i * (i + 1) / 2.0 for i in range(8)]
 MASS = [2.0 / (2.0 * i + 1.0) for i in range(8)]
 SYM = [[0, 3, 4], [3, 1, 5], [4, 5, 2]]
@@ -85,9 +86,12 @@
     return jnp.maximum(lev, i) <= order
 
 
-def one_hot(first, count, target):
-    row = lax.broadcasted_iota(jnp.int32, (count, 128), 0) + first
-    return jnp.where(row == target, 1.0, 0.0).astype(BF)
+def lane_pick(get, count, target):
+    low, tile = target & 127, target >> 7
+    out = jnp.zeros(target.shape, F32)
+    for t in range(count):
+        out = jnp.where(tile == t, jnp.take_along_axis(get(t), low, axis=1), out)
+    return out
 
 
 def point_pair(ge, go, q, r0, rows):
@@ -115,21 +119,61 @@
 def first_kernel(
     weights, wsum,
     order_hbm, u_hbm, v_hbm, send_hbm, grad_hbm, ztrace_hbm, wjk_hbm,
-    eu_ref, ab_ref, own_ref, tab_ref, visc_ref, vhi_ref, vlo_ref, s0_ref, s1_ref, s2_ref, s3_ref,
-    order_ref, u_ref, v_ref, send_ref, grad_ref, ztrace_ref, wjk_ref, ge, go, vm, sems,
+    eu_ref, ab_ref, own_ref, extra_ref, vhi_ref, vlo_ref, grad_ref, g0_ref, s0_ref, s1_ref, s2_ref, s3_ref,
+    order_ref, u_ref, v_ref, send_ref, ztrace_ref, wjk_ref, ge, go, sems,
 ):
-    names = ("order", "u", "grad", "v", "wjk", "ztrace", "send")
+    names = ("order", "v", "ztrace", "u", "grad", "send", "wjk")
     ends = (
-        (order_hbm, order_ref), (u_hbm, u_ref), (grad_hbm, grad_ref), (v_hbm, v_ref),
-        (wjk_hbm, wjk_ref), (ztrace_hbm, ztrace_ref), (send_hbm, send_ref),
+        (order_hbm, order_ref), (v_hbm, v_ref), (ztrace_hbm, ztrace_ref), (u_hbm, u_ref), (grad_hbm, grad_ref),
+        (send_hbm, send_ref), (wjk_hbm, wjk_ref),
     )
     loads = {n: pltpu.make_async_copy(*e, sems.at[k]) for k, (n, e) in enumerate(zip(names, ends))}
     for n in names:
         loads[n].start()
     loads["order"].wait()
-    loads["u"].wait()
     order = order_ref[...]
     lev = level()
+    loads["v"].wait()
+    for i in range(8):
+        live = alive(lev, i, order)
+        for c in range(3):
+            at = pl.ds(c * 512 + i * 64, 64)
+            value = jnp.where(live, v_ref[at, :], 0.0)
+            v_ref[at, :] = value
+            vhi_ref[at, :], vlo_ref[at, :] = split(value)
+
+    def put(c, row, rows, d, even_v, odd_v, even_g, odd_g):
+        for s in range(2):
+            lanes = pl.ds((2 * d + s) * 128, 128)
+            own_ref[pl.ds(c * 64 + row, rows), lanes] = even_v + odd_v if s else even_v - odd_v
+            own_ref[pl.ds(192 + c * 64 + row, rows), lanes] = even_g + odd_g if s else even_g - odd_g
+
+    def sums(get):
+        v = [get(i) for i in range(8)]
+        return (
+            (v[0] + v[2]) + (v[4] + v[6]),
+            (v[1] + v[3]) + (v[5] + v[7]),
+            (3.0 * v[2] + 10.0 * v[4]) + 21.0 * v[6],
+            (v[1] + 6.0 * v[3]) + (15.0 * v[5] + 28.0 * v[7]),
+        )
+
+    for c in range(3):
+        for m in range(8):
+            put(c, m * 8, 8, 0, *sums(lambda i: v_ref[pl.ds(c * 512 + i * 64 + m * 8, 8), :]))
+        for i in range(8):
+            put(c, i * 8, 8, 1, *sums(lambda j: v_ref[pl.ds(c * 512 + i * 64 + j * 8, 8), :]))
+    loads["ztrace"].wait()
+    both = jnp.concatenate([r[pl.ds(c * 512, 512), :] for r in (vhi_ref, vlo_ref) for c in range(3)], axis=1)
+    z = dot(ztrace_ref[...], both)
+    for c in range(3):
+        block = z[:, c * 128 : (c + 1) * 128] + z[:, 384 + c * 128 : 512 + c * 128]
+        for s in range(2):
+            lanes = pl.ds((4 + s) * 128, 128)
+            own_ref[pl.ds(c * 64, 64), lanes] = block[s * 64 : (s + 1) * 64]
+            own_ref[pl.ds(192 + c * 64, 64), lanes] = block[128 + s * 64 : 192 + s * 64]
+
+    for n in ("u", "grad", "send", "wjk"):
+        loads[n].wait()
     us = [[], []]
     for i in range(8):
         live = alive(lev, i, order)
@@ -137,23 +181,26 @@
             jnp.where(live, u_ref[pl.ds(c * 512 + i * 64, 64), :].astype(F32), 0.0).astype(BF)
             for c in range(3)
         ]
-        us[i % 2].append(jnp.concatenate(row, axis=1))
-    loads["grad"].wait()
+        us[i % 2].append(jnp.concatenate(row + [vhi_ref[pl.ds(i * 64, 64), :]], axis=1))
     for par, out in ((0, ge), (1, go)):
         u = jnp.concatenate(us[par], axis=0)
-        out[...] = dot(grad_ref[par], jnp.concatenate([u, u], axis=0))
-
-    loads["v"].wait()
-    loads["wjk"].wait()
-    loads["ztrace"].wait()
-    loads["send"].wait()
-    for i in range(8):
-        live = alive(lev, i, order)
-        for c in range(3):
-            at = pl.ds(c * 512 + i * 64, 64)
-            value = jnp.where(live, v_ref[at, :], 0.0)
-            vm[at, :] = value
-            vhi_ref[at, :], vlo_ref[at, :] = split(value)
+        whole = dot(grad_ref[par], jnp.concatenate([u, u], axis=0))
+        out[...] = whole[:, :384]
+        g0_ref[par] = whole[:, 384:]
+
+    up_x, up_y = lax.axis_index("gx") % 2 == 0, lax.axis_index("gy") % 2 == 0
+    rows = [send_ref[0, 0, k : k + 1, :] for k in range(4)]
+    picks = [
+        jnp.where(up_y, rows[2], rows[3]),
+        jnp.where(up_y, rows[3], rows[2]),
+        jnp.where(up_x, rows[0], rows[1]),
+        jnp.where(up_x, rows[1], rows[0]),
+    ]
+    targets = [jnp.broadcast_to(p, (8, 128)) for p in picks]
+    outs = (s0_ref, s1_ref, s2_ref, s3_ref)
+    for target, out in zip(targets, outs):
+        for r in range(0, 384, 8):
+            out[pl.ds(r, 8), :] = lane_pick(lambda f: own_ref[pl.ds(r, 8), pl.ds(f * 128, 128)], 6, target)
 
     total = jnp.zeros((8, 128), F32)
     for q in range(4):
@@ -172,92 +219,57 @@
                 ab_ref[pl.ds(512 + here, 8), :] = (8.0 * w) * (inv * inv * inv)
             return acc
 
-        total = lax.fori_loop(0, 8, points, total, unroll=2)
+        total = lax.fori_loop(0, 8, points, total, unroll=4)
     visc = jnp.sum(total, axis=0, keepdims=True) * (1.0 / wsum)
-    visc_ref[...] = jnp.broadcast_to(visc, (8, 128))
-
-    def put(c, row, rows, d, even_v, odd_v, even_g, odd_g):
-        for s in range(2):
-            lanes = pl.ds((2 * d + s) * 128, 128)
-            t = even_v + odd_v if s else even_v - odd_v
-            g = even_g + odd_g if s else even_g - odd_g
-            own_ref[pl.ds(c * 64 + row, rows), lanes] = t
-            own_ref[pl.ds(192 + c * 64 + row, rows), lanes] = g * visc
-
-    def sums(get):
-        v = [get(i) for i in range(8)]
-        return (
-            (v[0] + v[2]) + (v[4] + v[6]),
-            (v[1] + v[3]) + (v[5] + v[7]),
-            (3.0 * v[2] + 10.0 * v[4]) + 21.0 * v[6],
-            (v[1] + 6.0 * v[3]) + (15.0 * v[5] + 28.0 * v[7]),
-        )
-
-    for c in range(3):
-        for m in range(8):
-            put(c, m * 8, 8, 0, *sums(lambda i: vm[pl.ds(c * 512 + i * 64 + m * 8, 8), :]))
-        for i in range(8):
-            put(c, i * 8, 8, 1, *sums(lambda j: vm[pl.ds(c * 512 + i * 64 + j * 8, 8), :]))
-    both = jnp.concatenate(
-        [jnp.concatenate([r[pl.ds(c * 512, 512), :] for c in range(3)], axis=1) for r in (vhi_ref, vlo_ref)], axis=0
-    )
-    zt = ztrace_ref[...]
-    z = dot(jnp.concatenate([zt, zt], axis=1), both)
-    for c in range(3):
-        for s in range(2):
-            lanes = pl.ds((4 + s) * 128, 128)
-            block = z[:, c * 128 : (c + 1) * 128]
-            own_ref[pl.ds(c * 64, 64), lanes] = block[s * 64 : (s + 1) * 64]
-            own_ref[pl.ds(192 + c * 64, 64), lanes] = block[128 + s * 64 : 192 + s * 64] * visc
-
-    for f in range(6):
-        lanes = pl.ds(f * 128, 128)
-        for r in range(0, 384, 64):
-            hi, lo = split(own_ref[pl.ds(r, 64), lanes])
-            tab_ref[pl.ds(r, 64), lanes] = hi
-            tab_ref[pl.ds(r, 64), pl.ds(768 + f * 128, 128)] = lo
-    row = lax.broadcasted_iota(jnp.int32, (16, 128), 0)
+    row = lax.broadcasted_iota(jnp.int32, (8, 128), 0)
     extra = jnp.where(row == 0, visc, jnp.where(row == 1, order.astype(F32), 0.0))
-    hi, lo = split(extra)
-    for f in range(6):
-        tab_ref[pl.ds(384, 16), pl.ds(f * 128, 128)] = hi
-        tab_ref[pl.ds(384, 16), pl.ds(768 + f * 128, 128)] = lo
-
-    up_x, up_y = lax.axis_index("gx") % 2 == 0, lax.axis_index("gy") % 2 == 0
-    rows = [send_ref[0, 0, k : k + 1, :] for k in range(4)]
-    picks = [
-        jnp.where(up_y, rows[2], rows[3]),
-        jnp.where(up_y, rows[3], rows[2]),
-        jnp.where(up_x, rows[0], rows[1]),
-        jnp.where(up_x, rows[1], rows[0]),
-    ]
-    hot = jnp.concatenate([one_hot(0, 768, p) for p in picks], axis=1)
-    packet = dot(tab_ref[...], jnp.concatenate([hot, hot], axis=0))
-    for k, out in enumerate((s0_ref, s1_ref, s2_ref, s3_ref)):
-        out[...] = packet[:392, k * 128 : (k + 1) * 128]
+    extra_ref[...] = extra
+    for target, out in zip(targets, outs):
+        low = jnp.take_along_axis(extra, target & 127, axis=1)
+        out[pl.ds(384, 8), :] = jnp.where(target < 768, low, 0.0)
 
 
 def volume_kernel(
-    vhi_ref, vlo_ref, eu_ref, ab_ref, grad_ref, div_hbm, tab_ref, links_ref,
-    vol_ref, far_ref,
+    vhi_ref, vlo_ref, eu_ref, ab_ref, grad_ref, g0_ref, div_hbm, own_ref, extra_ref, links_ref,
+    vol_ref, far_ref, hot_ref, pick_ref,
     div_ref, ge, go, sp, sem,
 ):
     load = pltpu.make_async_copy(div_hbm, div_ref, sem)
     load.start()
+
+    def far(f):
+        target = jnp.broadcast_to(links_ref[f], (8, 128))
+        lanes = pl.ds(f * 128, 128)
+        for r in range(0, 384, 8):
+            far_ref[pl.ds(r, 8), lanes] = lane_pick(
+                lambda t: own_ref[pl.ds(r, 8), pl.ds(t * 128, 128)], 6, target
+            )
+        low = jnp.take_along_axis(extra_ref[...], target & 127, axis=1)
+        far_ref[pl.ds(384, 8), lanes] = jnp.where(target < 768, low, 0.0)
+        slot = target - 768
+        k = slot >> 7
+        block = jnp.where(k < 2, 2 + (k ^ flip_x), (k - 2) ^ flip_y)
+        target = jnp.where((slot < 0) | (slot >= 512), -1, block * 128 + (slot & 127))
+        pick_ref[f] = target
+        row = lax.broadcasted_iota(jnp.int32, (512, 128), 0)
+        hot_ref[:, lanes] = jnp.where(row == target[0:1, :], 1.0, 0.0).astype(BF)
+
+    flip_x, flip_y = lax.axis_index("gx") % 2, lax.axis_index("gy") % 2
+
+    def modes(ref, par, comps):
+        rows = [
+            jnp.concatenate([ref[pl.ds(c * 512 + i * 64, 64), :] for c in comps], axis=1) for i in range(par, 8, 2)
+        ]
+        return jnp.concatenate(rows, axis=0)
+
     for par, out in ((0, ge), (1, go)):
-        hi, lo = (
-            jnp.concatenate(
-                [
-                    jnp.concatenate([r[pl.ds(c * 512 + i * 64, 64), :] for c in range(3)], axis=1)
-                    for i in range(par, 8, 2)
-                ],
-                axis=0,
-            )
-            for r in (vhi_ref, vlo_ref)
-        )
+        hi, lo = modes(vhi_ref, par, (1, 2)), modes(vlo_ref, par, (1, 2))
         mat = grad_ref[par]
         left = jnp.concatenate([mat[:, :256], mat], axis=1)
-        out[...] = dot(left, jnp.concatenate([hi, lo, hi], axis=0))
+        out[:, 128:] = dot(left, jnp.concatenate([hi, lo, hi], axis=0))
+        out[:, :128] = g0_ref[par] + dot(mat[:, :256], modes(vlo_ref, par, (0,)))
+    for f in range(3):
+        far(f)
 
     for q in range(4):
 
@@ -283,60 +295,54 @@
                         sp[pl.ds(pl.multiple_of(base + r0, 16), 16), :] = piece
             return carry
 
-        lax.fori_loop(0, 4, points, 0)
+        lax.fori_loop(0, 4, points, 0, unroll=2)
 
     load.wait()
+
+    def stress(par, j, comps):
+        rows = []
+        for d in range(3):
+            k = (1 if d == 0 else 0) ^ par
+            cols = [sp[pl.ds(((SYM[d][c] * 2 + k) * 2 + j) * 256, 256), :] for c in comps]
+            rows.append(jnp.concatenate(cols, axis=1))
+        return jnp.concatenate(rows, axis=0)
+
     for par in range(2):
-        halves = []
-        for j in range(2):
-            rows = []
-            for d in range(3):
-                k = (1 if d == 0 else 0) ^ par
-                rows.append(
-                    jnp.concatenate(
-                        [sp[pl.ds(((SYM[d][c] * 2 + k) * 2 + j) * 256, 256), :] for c in range(3)], axis=1
-                    )
-                )
-            halves.append(jnp.concatenate(rows, axis=0))
         mat = div_ref[par]
+        hi, lo = stress(par, 0, (0, 1)), stress(par, 1, (0, 1))
         left = jnp.concatenate([mat[:, :768], mat], axis=1)
-        out = dot(left, jnp.concatenate([halves[0], halves[1], halves[0]], axis=0))
+        pair = dot(left, jnp.concatenate([hi, lo, hi], axis=0))
+        hi, lo = stress(par, 0, (2,)), stress(par, 1, (2,))
+        last = dot(mat[:, :768], jnp.concatenate([hi, lo], axis=1))
+        last = (last[:, :128] + last[:, 128:]) + dot(mat[:, 768:], hi)
         for ii in range(4):
-            for c in range(3):
-                vol_ref[pl.ds(c * 512 + (2 * ii + par) * 64, 64), :] = out[
-                    ii * 64 : ii * 64 + 64, c * 128 : c * 128 + 128
-                ]
-
-    hot = jnp.concatenate([one_hot(0, 768, links_ref[f]) for f in range(6)], axis=1)
-    far_ref[...] = dot(tab_ref[...], jnp.concatenate([hot, hot], axis=0))
+            for c, out in enumerate((pair[:, :128], pair[:, 128:], last)):
+                vol_ref[pl.ds(c * 512 + (2 * ii + par) * 64, 64), :] = out[ii * 64 : ii * 64 + 64]
+    for f in range(3, 6):
+        far(f)
 
 
 def face_kernel(
-    order_ref, far_ref, r0_ref, r1_ref, r2_ref, r3_ref, own_ref, visc_ref, links_ref, orient_ref,
+    order_ref, far_ref, hot_ref, pick_ref, r0_ref, r1_ref, r2_ref, r3_ref, own_ref, extra_ref, links_ref, orient_ref,
     vol_ref, zlift_ref, mab_ref,
     out_ref,
     got, acc, zin,
 ):
     order = order_ref[...]
-    his, los = [], []
-    for r in (r0_ref, r1_ref, r2_ref, r3_ref):
-        hi, lo = split(jnp.concatenate([r[...], jnp.zeros((8, 128), F32)], axis=0))
-        his.append(hi)
-        los.append(lo)
-    flip_x, flip_y = lax.axis_index("gx") % 2, lax.axis_index("gy") % 2
-    hots = []
+    blocks = (r0_ref, r1_ref, r2_ref, r3_ref)
+    parts = [split(r[pl.ds(0, MXU_ROWS), :]) for r in blocks]
+    left = jnp.concatenate([p[0] for p in parts] + [p[1] for p in parts], axis=1)
+    hot = hot_ref[...]
+    top = pl.ds(0, MXU_ROWS)
+    got[top, :] = far_ref[top, :] + dot(left, jnp.concatenate([hot, hot], axis=0))
     for f in range(6):
-        link = links_ref[f]
-        slot = link - 768
-        k = slot // 128
-        block = jnp.where(k < 2, 2 + (k ^ flip_x), (k - 2) ^ flip_y)
-        mapped = jnp.where((slot < 0) | (slot >= 512), -1, block * 128 + slot % 128)
-        hots.append(one_hot(0, 512, mapped))
-    hot = jnp.concatenate(hots, axis=1)
-    left = jnp.concatenate(his + los, axis=1)
-    got[...] = far_ref[...] + dot(left, jnp.concatenate([hot, hot], axis=0))
-
-    visc = visc_ref[0:1, :]
+        target = pick_ref[f]
+        lanes = pl.ds(f * 128, 128)
+        for r in range(MXU_ROWS, 392, 8):
+            at = (pl.ds(r, 8), lanes)
+            got[at] = far_ref[at] + lane_pick(lambda t: blocks[t][pl.ds(r, 8), :], 4, target)
+
+    visc = extra_ref[0:1, :]
     odd_b = lax.broadcasted_iota(jnp.int32, (8, 128), 0) % 2 == 1
     orderf = order.astype(F32)
     face = []
@@ -350,15 +356,15 @@
         share = jnp.where(links_ref[f] == 1280, 1.0, 0.5)
         top = jnp.maximum(orderf, far_order) + 1.0
         penalty = 2.0 * top * top * jnp.maximum(visc, far_visc)
-        face.append((lanes, spin, share, penalty, share * visc))
+        face.append((lanes, spin, share, penalty, share * visc, share * far_visc))
 
     def flux(f, c, a):
-        lanes, spin, share, penalty, weak = face[f]
+        lanes, spin, share, penalty, weak, weak_far = face[f]
         row, row_h = pl.ds(c * 64 + a * 8, 8), pl.ds(192 + c * 64 + a * 8, 8)
         rot = spin[a % 2]
         mm = mab_ref[pl.ds(a * 8, 8), :]
         jump = own_ref[row, lanes] - rot * got[row, lanes]
-        value = mm * (penalty * jump - share * (own_ref[row_h, lanes] - rot * got[row_h, lanes]))
+        value = mm * (penalty * jump - (weak * own_ref[row_h, lanes] - weak_far * (rot * got[row_h, lanes])))
         return value, mm * (-weak * jump)
 
     def pair(d, c, a):
@@ -372,8 +378,8 @@
             for k in range(4):
                 zin[pl.ds(k * 64 + a * 8, 8), pl.ds(c * 128, 128)] = parts[k]
     hi, lo = split(zin[...])
-    zl = zlift_ref[...]
-    acc[...] = dot(jnp.concatenate([zl, zl], axis=1), jnp.concatenate([hi, lo], axis=0))
+    lift = dot(zlift_ref[...], jnp.concatenate([hi, lo], axis=1))
+    acc[...] = lift[:, :384] + lift[:, 384:]
 
     lev = level()
     for c in range(3):
@@ -436,24 +442,23 @@
     v = adjoint_field.reshape(1536, 128)
     grad, div = jnp.asarray(tab["grad"]), jnp.asarray(tab["div"])
     links, turns = face_links.reshape(6, 1, 128), orient.reshape(6, 1, 128)
-    eu, ab, own, table, visc, vhi, vlo, *packets = pl.pallas_call(
+    eu, ab, own, extra, vhi, vlo, grad, g0, *packets = pl.pallas_call(
         functools.partial(first_kernel, tab["w"], tab["wsum"]),
-        out_shape=[shape(3072), shape(1024), shape(384, 768), shape(400, 1536, BF), shape(8)]
+        out_shape=[shape(3072), shape(1024), shape(384, 768), shape(8)]
         + [shape(1536, 128, BF)] * 2
+        + [jax.ShapeDtypeStruct((2, 768, 512), BF), jax.ShapeDtypeStruct((2, 768, 128), F32)]
         + [shape(392)] * 4,
         in_specs=[HBM] * 7,
-        out_specs=[VM] * 11,
+        out_specs=[VM] * 12,
         scratch_shapes=[
             pltpu.VMEM((1, 128), jnp.int32),
             pltpu.VMEM((1536, 128), BF),
             pltpu.VMEM((1536, 128), F32),
             pltpu.VMEM((1, 1, 4, 128), jnp.int32),
-            pltpu.VMEM((2, 768, 512), BF),
             pltpu.VMEM((256, 512), BF),
             pltpu.VMEM((64, 128), F32),
             pltpu.VMEM((768, 384), F32),
             pltpu.VMEM((768, 384), F32),
-            pltpu.VMEM((1536, 128), F32),
             pltpu.SemaphoreType.DMA((7,)),
         ],
         compiler_params=PARAMS,
@@ -465,25 +470,30 @@
         exchange(packets[2], "gx", 0),
         exchange(packets[3], "gx", 1),
     ]
-    vol, far = pl.pallas_call(
+    vol, far, hot, pick = pl.pallas_call(
         volume_kernel,
-        out_shape=[shape(1536), shape(400, 768)],
-        in_specs=[VM] * 5 + [HBM] + [VM] * 2,
-        out_specs=[VM] * 2,
+        out_shape=[
+            shape(1536),
+            shape(392, 768),
+            shape(512, 768, BF),
+            jax.ShapeDtypeStruct((6, 8, 128), jnp.int32),
+        ],
+        in_specs=[VM] * 6 + [HBM] + [VM] * 3,
+        out_specs=[VM] * 4,
         scratch_shapes=[pltpu.VMEM((2, 256, 1536), BF), pltpu.VMEM((768, 384), F32), pltpu.VMEM((768, 384), F32), pltpu.VMEM((6144, 128), BF), pltpu.SemaphoreType.DMA],
         compiler_params=PARAMS,
         name="volume",
-    )(vhi, vlo, eu, ab, grad, in_hbm(div), table, links)
+    )(vhi, vlo, eu, ab, grad, g0, in_hbm(div), own, extra, links)
     out = pl.pallas_call(
         face_kernel,
         out_shape=shape(1536),
-        in_specs=[VM] * 13,
+        in_specs=[VM] * 15,
         out_specs=VM,
-        scratch_shapes=[pltpu.VMEM((400, 768), F32), pltpu.VMEM((512, 384), F32), pltpu.VMEM((256, 384), F32)],
+        scratch_shapes=[pltpu.VMEM((392, 768), F32), pltpu.VMEM((512, 384), F32), pltpu.VMEM((256, 384), F32)],
         compiler_params=PARAMS,
         name="faces",
     )(
-        order, far, *got, own, visc, links, turns, vol,
+        order, far, hot, pick, *got, own, extra, links, turns, vol,
         jnp.asarray(tab["zlift"]), jnp.asarray(tab["mab"]),
     )
     return out.reshape(1, 1, 3, 512, 128)

time: 19.4 us -> 16.4 us (0.85)
  Pallas kernels: 13.3 us -> 9.65 us
  waiting for transfers between devices: 0.01 us -> 0.83 us
    pallas_call x2, Pallas kernels: 8.58 us -> 5.77 us  [the longest x1 3.55 us: body(): pl.pallas_call(volume_kernel, out_shape=[shape(1536), shape(392, 768), sh...]
    pallas_call x1, Pallas kernels: 4.75 us -> 3.89 us  [body(): pl.pallas_call(functools.partial(first_kernel, tab['w'], tab['wsum']), ou...]
    ppermute x4, waiting for transfers between devices: 0.01 us -> 0.83 us  [exchange(): return lax.ppermute(value, ('gx', 'gy'), links)]
  transfers between devices with their start and end apart: 4 -> 4, of which waited for: 0 -> 1; matrix products, arithmetic and copies ran while one was open for 0% -> 0% of each run, Pallas kernels for 30% -> 22%
where the time goes in v2:
time: 16.4 us; the launch traced here: 16.3 us
  Pallas kernels  9.65 us (59%)
  starting transfers between devices  5.69 us (35%)
  waiting for transfers between devices  0.83 us (5%)
    ppermute x4, starting transfers between devices, exchange(): return lax.ppermute(value, ('gx', 'gy'), links)  5.69 us
    pallas_call x1, Pallas kernels, body(): pl.pallas_call(functools.partial(first_kernel, tab['w'], tab['wsum']), ou...  3.89 us
    pallas_call x1, Pallas kernels, body(): pl.pallas_call(volume_kernel, out_shape=[shape(1536), shape(392, 768), sh...  3.55 us
    pallas_call x1, Pallas kernels, body(): pl.pallas_call(face_kernel, out_shape=shape(1536), in_specs=[VM] * 15, ou...  2.22 us
    ppermute x4, waiting for transfers between devices, exchange(): return lax.ppermute(value, ('gx', 'gy'), links)  0.83 us
  transfers between devices with their start and end apart: 4, of which 1 were waited for; matrix products, arithmetic and copies ran while one was open for 0% of the time, Pallas kernels for 22%

profile of v2, /device:TPU:0, one launch (start us, length us, event | category | flops | bytes accessed | tf_op | source)
XLA Modules:
  0.0 16.3 jit_solution(8382251995796815788)
XLA Ops:
  0.0 0.0 copy-start.2
  0.0 3.9 %state_and_traces.1 = (f32[3072,128]{1,0:T(8,128)S(1)}, f32[1024,128]{1,0:T(8,128)S(1)}, f32[384,768]{1,0:T(8,128)S(1)}, f32[8,128]{1,0:T(8,128)S(1)}, bf16[1536...) custom-call(s32[1,128]{1,0:T(1,128)} %bitcast.9, ...), custom_call_target="tpu_custom_call" | custom-call | tf_op jit(solution)/shard_map/state_and_traces/pallas_call | solution.py:445
  3.9 0.6 %collective-permute-start = (f32[392,128]{1,0:T(8,128)S(1)}, f32[392,128]{1,0:T(8,128)S(1)}, u32[]{:S(2)}, u32[]{:S(2)}) collective-permute-start(f32[392,128]{1,0:T(8,128)S(1)} %get-tuple-element.32), channel_id=1, source_target_pairs={{0,1},{1,0},{2,3},{3,2},{4,5},{5,4},{6,7},{7,6},{8,9},{9,8},{10,11... | collective-permute-start | bytes 602120 | tf_op jit(solution)/shard_map/ppermute | solution.py:431
  4.5 3.5 %collective-permute-start.1 = (f32[392,128]{1,0:T(8,128)S(1)}, f32[392,128]{1,0:T(8,128)S(1)}, u32[]{:S(2)}, u32[]{:S(2)}) collective-permute-start(f32[392,128]{1,0:T(8,128)S(1)} %get-tuple-element.33), channel_id=1, source_target_pairs={{0,7},{1,2},{2,1},{3,4},{4,3},{5,6},{6,5},{7,0},{8,15},{9,10},{10,... | collective-permute-start | bytes 602120 | tf_op jit(solution)/shard_map/ppermute | solution.py:431
  8.0 1.6 %collective-permute-start.2 = (f32[392,128]{1,0:T(8,128)S(1)}, f32[392,128]{1,0:T(8,128)S(1)}, u32[]{:S(2)}, u32[]{:S(2)}) collective-permute-start(f32[392,128]{1,0:T(8,128)S(1)} %get-tuple-element.34), channel_id=1, source_target_pairs={{0,8},{1,9},{2,10},{3,11},{4,12},{5,13},{6,14},{7,15},{8,0},{9,1},... | collective-permute-start | bytes 602120 | tf_op jit(solution)/shard_map/ppermute | solution.py:431
  9.6 0.0 collective-permute-start.3
  9.6 0.0 copy-done.2
  9.6 0.0 copy-start
  9.6 0.0 copy-start.1
  9.6 0.0 copy-start.3
  9.6 0.0 copy-start.4
  9.6 3.5 %volume.1 = (f32[1536,128]{1,0:T(8,128)S(1)}, f32[392,768]{1,0:T(8,128)S(1)}, bf16[512,768]{1,0:T(8,128)(2,1)S(1)}, s32[6,8,128]{2,1,0:T(8,128)S(1)}) custom-call(bf16[1536,128]{1,0:T(8,128)(2,1)S(1)} %get-tuple-element.21.vhi_ref, bf16[1536,128]{1,0:T(8,128)(2,1)S(1)} %get-tuple-element.22.vlo_ref, f32[3072,128]{1,0:T(8,128)S(1)} %get-tuple-element.23.eu_ref, ...), custom_call_target="tpu_custom_call" | custom-call | tf_op jit(solution)/shard_map/volume/pallas_call | solution.py:473
  13.2 0.0 collective-permute-done.r0_ref
  13.2 0.0 collective-permute-done.1.r1_ref
  13.2 0.8 %collective-permute-done.2.r2_ref = f32[392,128]{1,0:T(8,128)S(1)} collective-permute-done((f32[392,128]{1,0:T(8,128)S(1)}, f32[392,128]{1,0:T(8,128)S(1)}, u32[]{:S(2)}, u32[]{:S(2)}) %collective-permute-start.2) | collective-permute-done | bytes 200736 | tf_op jit(solution)/shard_map/ppermute | solution.py:431
  14.0 0.0 collective-permute-done.3.r3_ref
  14.0 0.0 copy-done
  14.0 0.0 copy-done.1
  14.0 0.0 copy-done.3
  14.0 0.0 copy-done.4
  14.1 2.2 %faces.1 = f32[1536,128]{1,0:T(8,128)} custom-call(s32[1,128]{1,0:T(1,128)S(1)} %bitcast.10, f32[392,768]{1,0:T(8,128)S(1)} %get-tuple-element.29.far_ref, bf16[512,768]{1,0:T(8,128)(2,1)S(1)} %get-tuple-element.30.hot_ref, s32[6,8,128]{2,1,0:T(8,128)S(1)} %get-tuple-element.31.pick_ref, f32[392,128]{1,0:T(8,128)S(1)} %collective-permute-done.r0_ref, ...), custom_call_target="tpu_custom_call" | custom-call | tf_op jit(solution)/shard_map/faces/pallas_call | solution.py:487
Async XLA Ops:
  0.0 9.6 %copy-start.2 = (s32[1,1,6,128]{3,1,2,0:T(1,128)S(1)}, s32[1,1,6,128]{3,1,2,0:T(1,128)}, u32[]{:S(2)}) copy-start(s32[1,1,6,128]{3,1,2,0:T(1,128)} %param.15) | copy-start | bytes 9220
  3.9 9.3 %collective-permute-start = (f32[392,128]{1,0:T(8,128)S(1)}, f32[392,128]{1,0:T(8,128)S(1)}, u32[]{:S(2)}, u32[]{:S(2)}) collective-permute-start(f32[392,128]{1,0:T(8,128)S(1)} %get-tuple-element.32), channel_id=1, source_target_pairs={{0,1},{1,0},{2,3},{3,2},{4,5},{5,4},{6,7},{7,6},{8,9},{9,8},{10,11... | collective-permute-start | bytes 602120 | tf_op jit(solution)/shard_map/ppermute | solution.py:431
  4.5 8.7 %collective-permute-start.1 = (f32[392,128]{1,0:T(8,128)S(1)}, f32[392,128]{1,0:T(8,128)S(1)}, u32[]{:S(2)}, u32[]{:S(2)}) collective-permute-start(f32[392,128]{1,0:T(8,128)S(1)} %get-tuple-element.33), channel_id=1, source_target_pairs={{0,7},{1,2},{2,1},{3,4},{4,3},{5,6},{6,5},{7,0},{8,15},{9,10},{10,... | collective-permute-start | bytes 602120 | tf_op jit(solution)/shard_map/ppermute | solution.py:431
  8.0 6.0 %collective-permute-start.2 = (f32[392,128]{1,0:T(8,128)S(1)}, f32[392,128]{1,0:T(8,128)S(1)}, u32[]{:S(2)}, u32[]{:S(2)}) collective-permute-start(f32[392,128]{1,0:T(8,128)S(1)} %get-tuple-element.34), channel_id=1, source_target_pairs={{0,8},{1,9},{2,10},{3,11},{4,12},{5,13},{6,14},{7,15},{8,0},{9,1},... | collective-permute-start | bytes 602120 | tf_op jit(solution)/shard_map/ppermute | solution.py:431
  9.6 4.4 %collective-permute-start.3 = (f32[392,128]{1,0:T(8,128)S(1)}, f32[392,128]{1,0:T(8,128)S(1)}, u32[]{:S(2)}, u32[]{:S(2)}) collective-permute-start(f32[392,128]{1,0:T(8,128)S(1)} %get-tuple-element.35), channel_id=1, source_target_pairs={{0,1},{1,0},{2,3},{3,2},{4,5},{5,4},{6,7},{7,6},{8,16},{9,17},{10,... | collective-permute-start | bytes 602120 | tf_op jit(solution)/shard_map/ppermute | solution.py:431
  9.6 4.4 %copy-start = (bf16[512,256]{1,0:T(8,128)(2,1)S(1)}, bf16[512,256]{1,0:T(8,128)(2,1)}, u32[]{:S(2)}) copy-start(bf16[512,256]{1,0:T(8,128)(2,1)} %constant.16.clone.zlift_ref) | copy-start | bytes 786436
  9.6 4.4 %copy-start.1 = (f32[64,128]{1,0:T(8,128)S(1)}, f32[64,128]{1,0:T(8,128)}, u32[]{:S(2)}) copy-start(f32[64,128]{1,0:T(8,128)} %constant.17.clone.mab_ref) | copy-start | bytes 98308
  9.6 4.4 %copy-start.3 = (s32[1,1,6,128]{3,1,2,0:T(1,128)S(1)}, s32[1,1,6,128]{3,1,2,0:T(1,128)}, u32[]{:S(2)}) copy-start(s32[1,1,6,128]{3,1,2,0:T(1,128)} %param.16) | copy-start | bytes 9220
  9.6 4.4 %copy-start.4 = (s32[1,1,128]{2,1,0:T(1,128)S(1)}, s32[1,1,128]{2,1,0:T(1,128)}, u32[]{:S(2)}) copy-start(s32[1,1,128]{2,1,0:T(1,128)} %param.12) | copy-start | bytes 1540

commit v3 on v2

--- a/solution.py
+++ b/solution.py
@@ -94,11 +94,15 @@
     return out
 
 
+def aligned(x):
+    return x if isinstance(x, int) else pl.multiple_of(x, 8)
+
+
 def point_pair(ge, go, q, r0, rows):
     even, odd = {}, {}
     for d in range(3):
         for c in range(3):
-            at = (pl.ds(pl.multiple_of(d * 256 + q * 64 + r0, 8), rows), pl.ds(c * 128, 128))
+            at = (pl.ds(aligned(d * 256 + q * 64 + r0), rows), pl.ds(c * 128, 128))
             even[d, c], odd[d, c] = ge[at], go[at]
 
     def strain(g):
@@ -122,10 +126,10 @@
     eu_ref, ab_ref, own_ref, extra_ref, vhi_ref, vlo_ref, grad_ref, g0_ref, s0_ref, s1_ref, s2_ref, s3_ref,
     order_ref, u_ref, v_ref, send_ref, ztrace_ref, wjk_ref, ge, go, sems,
 ):
-    names = ("order", "v", "ztrace", "u", "grad", "send", "wjk")
+    names = ("order", "v", "ztrace", "send", "u", "wjk", "grad0", "grad1")
     ends = (
-        (order_hbm, order_ref), (v_hbm, v_ref), (ztrace_hbm, ztrace_ref), (u_hbm, u_ref), (grad_hbm, grad_ref),
-        (send_hbm, send_ref), (wjk_hbm, wjk_ref),
+        (order_hbm, order_ref), (v_hbm, v_ref), (ztrace_hbm, ztrace_ref), (send_hbm, send_ref), (u_hbm, u_ref),
+        (wjk_hbm, wjk_ref), (grad_hbm.at[0], grad_ref.at[0]), (grad_hbm.at[1], grad_ref.at[1]),
     )
     loads = {n: pltpu.make_async_copy(*e, sems.at[k]) for k, (n, e) in enumerate(zip(names, ends))}
     for n in names:
@@ -163,6 +167,7 @@
         for i in range(8):
             put(c, i * 8, 8, 1, *sums(lambda j: v_ref[pl.ds(c * 512 + i * 64 + j * 8, 8), :]))
     loads["ztrace"].wait()
+    loads["send"].wait()
     both = jnp.concatenate([r[pl.ds(c * 512, 512), :] for r in (vhi_ref, vlo_ref) for c in range(3)], axis=1)
     z = dot(ztrace_ref[...], both)
     for c in range(3):
@@ -171,22 +176,6 @@
             lanes = pl.ds((4 + s) * 128, 128)
             own_ref[pl.ds(c * 64, 64), lanes] = block[s * 64 : (s + 1) * 64]
             own_ref[pl.ds(192 + c * 64, 64), lanes] = block[128 + s * 64 : 192 + s * 64]
-
-    for n in ("u", "grad", "send", "wjk"):
-        loads[n].wait()
-    us = [[], []]
-    for i in range(8):
-        live = alive(lev, i, order)
-        row = [
-            jnp.where(live, u_ref[pl.ds(c * 512 + i * 64, 64), :].astype(F32), 0.0).astype(BF)
-            for c in range(3)
-        ]
-        us[i % 2].append(jnp.concatenate(row + [vhi_ref[pl.ds(i * 64, 64), :]], axis=1))
-    for par, out in ((0, ge), (1, go)):
-        u = jnp.concatenate(us[par], axis=0)
-        whole = dot(grad_ref[par], jnp.concatenate([u, u], axis=0))
-        out[...] = whole[:, :384]
-        g0_ref[par] = whole[:, 384:]
 
     up_x, up_y = lax.axis_index("gx") % 2 == 0, lax.axis_index("gy") % 2 == 0
     rows = [send_ref[0, 0, k : k + 1, :] for k in range(4)]
@@ -198,28 +187,52 @@
     ]
     targets = [jnp.broadcast_to(p, (8, 128)) for p in picks]
     outs = (s0_ref, s1_ref, s2_ref, s3_ref)
-    for target, out in zip(targets, outs):
+
+    def pack(k):
         for r in range(0, 384, 8):
-            out[pl.ds(r, 8), :] = lane_pick(lambda f: own_ref[pl.ds(r, 8), pl.ds(f * 128, 128)], 6, target)
+            outs[k][pl.ds(r, 8), :] = lane_pick(
+                lambda f: own_ref[pl.ds(r, 8), pl.ds(f * 128, 128)], 6, targets[k]
+            )
+
+    pack(0)
+    for n in ("u", "wjk", "grad0", "grad1"):
+        loads[n].wait()
+    us = [[], []]
+    for i in range(8):
+        live = alive(lev, i, order)
+        row = [
+            jnp.where(live, u_ref[pl.ds(c * 512 + i * 64, 64), :].astype(F32), 0.0).astype(BF)
+            for c in range(3)
+        ]
+        us[i % 2].append(jnp.concatenate(row + [vhi_ref[pl.ds(i * 64, 64), :]], axis=1))
+    pack(1)
+    for par, out in ((0, ge), (1, go)):
+        u = jnp.concatenate(us[par], axis=0)
+        whole = dot(grad_ref[par], jnp.concatenate([u, u], axis=0))
+        out[...] = whole[:, :384]
+        g0_ref[par] = whole[:, 384:]
+    pack(2)
+    pack(3)
 
     total = jnp.zeros((8, 128), F32)
     for q in range(4):
 
         def points(m, acc, q=q):
-            r0 = pl.multiple_of(m * 8, 8)
+            r0 = m * 8
             w = wjk_ref[pl.ds(r0, 8), :] * weights[q]
             for at, e in zip((q, 7 - q), point_pair(ge, go, q, r0, 8)):
                 inv = lax.rsqrt(2.0 * contract(e, e) + DELTA * DELTA)
                 wmu = w + (2.0 * w) * inv
                 acc = acc + wmu
-                here = pl.multiple_of(at * 64 + r0, 8)
+                here = at * 64 + r0
                 for s in range(6):
                     eu_ref[pl.ds(s * 512 + here, 8), :] = e[s]
                 ab_ref[pl.ds(here, 8), :] = 2.0 * wmu
                 ab_ref[pl.ds(512 + here, 8), :] = (8.0 * w) * (inv * inv * inv)
             return acc
 
-        total = lax.fori_loop(0, 8, points, total, unroll=4)
+        for m in range(8):
+            total = points(m, total)
     visc = jnp.sum(total, axis=0, keepdims=True) * (1.0 / wsum)
     row = lax.broadcasted_iota(jnp.int32, (8, 128), 0)
     extra = jnp.where(row == 0, visc, jnp.where(row == 1, order.astype(F32), 0.0))
@@ -229,9 +242,15 @@
         out[pl.ds(384, 8), :] = jnp.where(target < 768, low, 0.0)
 
 
+def face_signs(bits):
+    odd_b = lax.broadcasted_iota(jnp.int32, (8, 128), 0) % 2 == 1
+    second = jnp.where(odd_b & (bits >= 2), -1.0, 1.0)
+    return second, second * jnp.where(bits % 2 == 1, -1.0, 1.0)
+
+
 def volume_kernel(
-    vhi_ref, vlo_ref, eu_ref, ab_ref, grad_ref, g0_ref, div_hbm, own_ref, extra_ref, links_ref,
-    vol_ref, far_ref, hot_ref, pick_ref,
+    vhi_ref, vlo_ref, eu_ref, ab_ref, grad_ref, g0_ref, div_hbm, own_ref, extra_ref, links_ref, orient_ref, mab_ref,
+    vol_ref, jump_ref, part_ref, aux_ref, hot_ref, pick_ref,
     div_ref, ge, go, sp, sem,
 ):
     load = pltpu.make_async_copy(div_hbm, div_ref, sem)
@@ -240,12 +259,20 @@
     def far(f):
         target = jnp.broadcast_to(links_ref[f], (8, 128))
         lanes = pl.ds(f * 128, 128)
-        for r in range(0, 384, 8):
-            far_ref[pl.ds(r, 8), lanes] = lane_pick(
-                lambda t: own_ref[pl.ds(r, 8), pl.ds(t * 128, 128)], 6, target
-            )
-        low = jnp.take_along_axis(extra_ref[...], target & 127, axis=1)
-        far_ref[pl.ds(384, 8), lanes] = jnp.where(target < 768, low, 0.0)
+        aux = jnp.where(target < 768, jnp.take_along_axis(extra_ref[...], target & 127, axis=1), 0.0)
+        aux_ref[f] = aux
+        spin = face_signs(orient_ref[f])
+        share = jnp.where(links_ref[f] == 1280, 1.0, 0.5)
+        weak, weak_far = share * extra_ref[0:1, :], share * aux[0:1, :]
+        for a in range(8):
+            mm = mab_ref[pl.ds(a * 8, 8), :]
+            own_part, far_part = mm * weak, mm * weak_far * spin[a % 2]
+            for c in range(3):
+                at, at_g = pl.ds(c * 64 + a * 8, 8), pl.ds(192 + c * 64 + a * 8, 8)
+                far_t = lane_pick(lambda t: own_ref[at, pl.ds(t * 128, 128)], 6, target)
+                far_g = lane_pick(lambda t: own_ref[at_g, pl.ds(t * 128, 128)], 6, target)
+                jump_ref[at, lanes] = own_ref[at, lanes] - spin[a % 2] * far_t
+                part_ref[at, lanes] = far_part * far_g - own_part * own_ref[at_g, lanes]
         slot = target - 768
         k = slot >> 7
         block = jnp.where(k < 2, 2 + (k ^ flip_x), (k - 2) ^ flip_y)
@@ -323,8 +350,8 @@
 
 
 def face_kernel(
-    order_ref, far_ref, hot_ref, pick_ref, r0_ref, r1_ref, r2_ref, r3_ref, own_ref, extra_ref, links_ref, orient_ref,
-    vol_ref, zlift_ref, mab_ref,
+    order_ref, jump_ref, part_ref, aux_ref, hot_ref, pick_ref, r0_ref, r1_ref, r2_ref, r3_ref, extra_ref,
+    links_ref, orient_ref, vol_ref, zlift_ref, mab_ref,
     out_ref,
     got, acc, zin,
 ):
@@ -333,47 +360,40 @@
     parts = [split(r[pl.ds(0, MXU_ROWS), :]) for r in blocks]
     left = jnp.concatenate([p[0] for p in parts] + [p[1] for p in parts], axis=1)
     hot = hot_ref[...]
-    top = pl.ds(0, MXU_ROWS)
-    got[top, :] = far_ref[top, :] + dot(left, jnp.concatenate([hot, hot], axis=0))
+    got[pl.ds(0, MXU_ROWS), :] = dot(left, jnp.concatenate([hot, hot], axis=0))
     for f in range(6):
-        target = pick_ref[f]
-        lanes = pl.ds(f * 128, 128)
         for r in range(MXU_ROWS, 392, 8):
-            at = (pl.ds(r, 8), lanes)
-            got[at] = far_ref[at] + lane_pick(lambda t: blocks[t][pl.ds(r, 8), :], 4, target)
+            got[pl.ds(r, 8), pl.ds(f * 128, 128)] = lane_pick(
+                lambda t: blocks[t][pl.ds(r, 8), :], 4, pick_ref[f]
+            )
 
     visc = extra_ref[0:1, :]
-    odd_b = lax.broadcasted_iota(jnp.int32, (8, 128), 0) % 2 == 1
     orderf = order.astype(F32)
     face = []
     for f in range(6):
         lanes = pl.ds(f * 128, 128)
-        bits = orient_ref[f]
-        first = jnp.where(bits % 2 == 1, -1.0, 1.0)
-        second = jnp.where(odd_b & (bits >= 2), -1.0, 1.0)
-        spin = (second, second * first)
-        far_visc, far_order = got[pl.ds(384, 1), lanes], got[pl.ds(385, 1), lanes]
+        spin = face_signs(orient_ref[f])
+        recv_visc, recv_order = got[pl.ds(384, 1), lanes], got[pl.ds(385, 1), lanes]
         share = jnp.where(links_ref[f] == 1280, 1.0, 0.5)
-        top = jnp.maximum(orderf, far_order) + 1.0
-        penalty = 2.0 * top * top * jnp.maximum(visc, far_visc)
-        face.append((lanes, spin, share, penalty, share * visc, share * far_visc))
+        top = jnp.maximum(orderf, aux_ref[f, 1:2, :] + recv_order) + 1.0
+        penalty = 2.0 * top * top * jnp.maximum(visc, aux_ref[f, 0:1, :] + recv_visc)
+        face.append((lanes, spin, penalty, share * visc, share * recv_visc))
 
     def flux(f, c, a):
-        lanes, spin, share, penalty, weak, weak_far = face[f]
-        row, row_h = pl.ds(c * 64 + a * 8, 8), pl.ds(192 + c * 64 + a * 8, 8)
-        rot = spin[a % 2]
+        lanes, spin, penalty, weak, weak_far = face[f]
+        row, row_g = pl.ds(c * 64 + a * 8, 8), pl.ds(192 + c * 64 + a * 8, 8)
         mm = mab_ref[pl.ds(a * 8, 8), :]
-        jump = own_ref[row, lanes] - rot * got[row, lanes]
-        value = mm * (penalty * jump - (weak * own_ref[row_h, lanes] - weak_far * (rot * got[row_h, lanes])))
-        return value, mm * (-weak * jump)
+        jump = jump_ref[row, lanes] - spin[a % 2] * got[row, lanes]
+        value = (mm * penalty) * jump + (part_ref[row, lanes] + (mm * weak_far * spin[a % 2]) * got[row_g, lanes])
+        return value, (mm * -weak) * jump
 
     def pair(d, c, a):
         v0, g0 = flux(2 * d, c, a)
         v1, g1 = flux(2 * d + 1, c, a)
         return v1 + v0, v1 - v0, g1 + g0, g1 - g0
 
-    for c in range(3):
-        for a in range(8):
+    for a in range(8):
+        for c in range(3):
             parts = pair(2, c, a)
             for k in range(4):
                 zin[pl.ds(k * 64 + a * 8, 8), pl.ds(c * 128, 128)] = parts[k]
@@ -382,21 +402,23 @@
     acc[...] = lift[:, :384] + lift[:, 384:]
 
     lev = level()
-    for c in range(3):
-        lanes = pl.ds(c * 128, 128)
-        for a in range(8):
+    for a in range(8):
+        for c in range(3):
+            lanes = pl.ds(c * 128, 128)
             ve, vo, ge, go = pair(1, c, a)
             for j in range(8):
                 at = pl.ds(a * 64 + j * 8, 8)
                 acc[at, lanes] = acc[at, lanes] + ((vo + SLOPE[j] * go) if j % 2 else (ve + SLOPE[j] * ge))
-        for a in range(8):
+    for a in range(8):
+        live = [alive(lev[a * 8 : a * 8 + 8], i, order) for i in range(8)]
+        for c in range(3):
+            lanes = pl.ds(c * 128, 128)
             ve, vo, ge, go = pair(0, c, a)
             for i in range(8):
                 at = pl.ds(i * 64 + a * 8, 8)
                 to = pl.ds(c * 512 + i * 64 + a * 8, 8)
                 value = acc[at, lanes] + ((vo + SLOPE[i] * go) if i % 2 else (ve + SLOPE[i] * ge))
-                live = alive(lev[a * 8 : a * 8 + 8], i, order)
-                out_ref[to, :] = jnp.where(live, vol_ref[to, :] + value, 0.0)
+                out_ref[to, :] = jnp.where(live[i], vol_ref[to, :] + value, 0.0)
 
 
 def shape(rows, cols=128, kind=F32):
@@ -440,6 +462,7 @@
     order = orders[0]
     u = velocity.reshape(1536, 128)
     v = adjoint_field.reshape(1536, 128)
+    mab = jnp.asarray(tab["mab"])
     grad, div = jnp.asarray(tab["grad"]), jnp.asarray(tab["div"])
     links, turns = face_links.reshape(6, 1, 128), orient.reshape(6, 1, 128)
     eu, ab, own, extra, vhi, vlo, grad, g0, *packets = pl.pallas_call(
@@ -459,7 +482,7 @@
             pltpu.VMEM((64, 128), F32),
             pltpu.VMEM((768, 384), F32),
             pltpu.VMEM((768, 384), F32),
-            pltpu.SemaphoreType.DMA((7,)),
+            pltpu.SemaphoreType.DMA((8,)),
         ],
         compiler_params=PARAMS,
         name="state_and_traces",
@@ -470,31 +493,37 @@
         exchange(packets[2], "gx", 0),
         exchange(packets[3], "gx", 1),
     ]
-    vol, far, hot, pick = pl.pallas_call(
+    vol, jump, part, aux, hot, pick = pl.pallas_call(
         volume_kernel,
         out_shape=[
             shape(1536),
-            shape(392, 768),
+            shape(192, 768),
+            shape(192, 768),
+            jax.ShapeDtypeStruct((6, 8, 128), F32),
             shape(512, 768, BF),
             jax.ShapeDtypeStruct((6, 8, 128), jnp.int32),
         ],
-        in_specs=[VM] * 6 + [HBM] + [VM] * 3,
-        out_specs=[VM] * 4,
+        in_specs=[VM] * 6 + [HBM] + [VM] * 5,
+        out_specs=[VM] * 6,
         scratch_shapes=[pltpu.VMEM((2, 256, 1536), BF), pltpu.VMEM((768, 384), F32), pltpu.VMEM((768, 384), F32), pltpu.VMEM((6144, 128), BF), pltpu.SemaphoreType.DMA],
         compiler_params=PARAMS,
         name="volume",
-    )(vhi, vlo, eu, ab, grad, g0, in_hbm(div), own, extra, links)
+    )(vhi, vlo, eu, ab, grad, g0, in_hbm(div), own, extra, links, turns, mab)
     out = pl.pallas_call(
         face_kernel,
         out_shape=shape(1536),
-        in_specs=[VM] * 15,
+        in_specs=[VM] * 16,
         out_specs=VM,
-        scratch_shapes=[pltpu.VMEM((392, 768), F32), pltpu.VMEM((512, 384), F32), pltpu.VMEM((256, 384), F32)],
+        scratch_shapes=[
+            pltpu.VMEM((392, 768), F32),
+            pltpu.VMEM((512, 384), F32),
+            pltpu.VMEM((256, 384), F32),
+        ],
         compiler_params=PARAMS,
         name="faces",
     )(
-        order, far, hot, pick, *got, own, extra, links, turns, vol,
-        jnp.asarray(tab["zlift"]), jnp.asarray(tab["mab"]),
+        order, jump, part, aux, hot, pick, *got, extra, links, turns, vol,
+        jnp.asarray(tab["zlift"]), mab,
     )
     return out.reshape(1, 1, 3, 512, 128)
 

time: 16.4 us -> 16 us (0.976)
  Pallas kernels: 9.65 us -> 9.19 us
    pallas_call x1, Pallas kernels: 3.89 us -> 3.39 us  [body(): pl.pallas_call(functools.partial(first_kernel, tab['w'], tab['wsum']), ou...]
where the time goes in v3:
time: 16 us; the launch traced here: 15.8 us
  Pallas kernels  9.19 us (57%)
  starting transfers between devices  5.72 us (36%)
  waiting for transfers between devices  0.84 us (5%)
    ppermute x4, starting transfers between devices, exchange(): return lax.ppermute(value, ('gx', 'gy'), links)  5.72 us
    pallas_call x1, Pallas kernels, body(): pl.pallas_call(volume_kernel, out_shape=[shape(1536), shape(192, 768), sh...  3.54 us
    pallas_call x1, Pallas kernels, body(): pl.pallas_call(functools.partial(first_kernel, tab['w'], tab['wsum']), ou...  3.39 us
    pallas_call x1, Pallas kernels, body(): pl.pallas_call(face_kernel, out_shape=shape(1536), in_specs=[VM] * 16, ou...  2.26 us
    ppermute x4, waiting for transfers between devices, exchange(): return lax.ppermute(value, ('gx', 'gy'), links)  0.84 us
  transfers between devices with their start and end apart: 4, of which 1 were waited for; matrix products, arithmetic and copies ran while one was open for 0% of the time, Pallas kernels for 22%

profile of v3, /device:TPU:0, one launch (start us, length us, event | category | flops | bytes accessed | tf_op | source)
XLA Modules:
  0.0 15.8 jit_solution(11717111711265656113)
XLA Ops:
  0.0 0.0 copy-start.1
  0.0 0.0 copy-start.3
  0.0 0.0 copy-start.2
  0.0 3.4 %state_and_traces.1 = (f32[3072,128]{1,0:T(8,128)S(1)}, f32[1024,128]{1,0:T(8,128)S(1)}, f32[384,768]{1,0:T(8,128)S(1)}, f32[8,128]{1,0:T(8,128)S(1)}, bf16[1536...) custom-call(s32[1,128]{1,0:T(1,128)} %bitcast.10, ...), custom_call_target="tpu_custom_call" | custom-call | tf_op jit(solution)/shard_map/state_and_traces/pallas_call | solution.py:468
  3.4 0.6 %collective-permute-start = (f32[392,128]{1,0:T(8,128)S(1)}, f32[392,128]{1,0:T(8,128)S(1)}, u32[]{:S(2)}, u32[]{:S(2)}) collective-permute-start(f32[392,128]{1,0:T(8,128)S(1)} %get-tuple-element.36), channel_id=1, source_target_pairs={{0,1},{1,0},{2,3},{3,2},{4,5},{5,4},{6,7},{7,6},{8,9},{9,8},{10,11... | collective-permute-start | bytes 602120 | tf_op jit(solution)/shard_map/ppermute | solution.py:453
  4.0 3.6 %collective-permute-start.1 = (f32[392,128]{1,0:T(8,128)S(1)}, f32[392,128]{1,0:T(8,128)S(1)}, u32[]{:S(2)}, u32[]{:S(2)}) collective-permute-start(f32[392,128]{1,0:T(8,128)S(1)} %get-tuple-element.37), channel_id=1, source_target_pairs={{0,7},{1,2},{2,1},{3,4},{4,3},{5,6},{6,5},{7,0},{8,15},{9,10},{10,... | collective-permute-start | bytes 602120 | tf_op jit(solution)/shard_map/ppermute | solution.py:453
  7.5 1.6 %collective-permute-start.2 = (f32[392,128]{1,0:T(8,128)S(1)}, f32[392,128]{1,0:T(8,128)S(1)}, u32[]{:S(2)}, u32[]{:S(2)}) collective-permute-start(f32[392,128]{1,0:T(8,128)S(1)} %get-tuple-element.38), channel_id=1, source_target_pairs={{0,8},{1,9},{2,10},{3,11},{4,12},{5,13},{6,14},{7,15},{8,0},{9,1},... | collective-permute-start | bytes 602120 | tf_op jit(solution)/shard_map/ppermute | solution.py:453
  9.1 0.0 collective-permute-start.3
  9.1 0.0 copy-done.1
  9.1 0.0 copy-done.3
  9.1 0.0 copy-done.2
  9.1 0.0 copy-start
  9.2 0.0 copy-start.4
  9.2 3.5 %volume.1 = (f32[1536,128]{1,0:T(8,128)S(1)}, f32[192,768]{1,0:T(8,128)S(1)}, f32[192,768]{1,0:T(8,128)S(1)}, f32[6,8,128]{2,1,0:T(8,128)S(1)}, bf16[512,768]{1,0:T(8,128)(2,1)S(1)}, /*index=5*/s32[6,8,128]{2,1,0:T(8,128)S(1)}) custom-call(bf16[1536,128]{1,0:T(8,128)(2,1)S(1)} %get-tuple-element.23.vhi_ref, bf16[1536,128]{1,0:T(8,128)(2,1)S(1)} %get-tuple-element.24.vlo_ref, ...), custom_call_target="tpu_custom_call" | custom-call | tf_op jit(solution)/shard_map/volume/pallas_call | solution.py:496
  12.7 0.0 collective-permute-done.r0_ref
  12.7 0.0 collective-permute-done.1.r1_ref
  12.7 0.8 %collective-permute-done.2.r2_ref = f32[392,128]{1,0:T(8,128)S(1)} collective-permute-done((f32[392,128]{1,0:T(8,128)S(1)}, f32[392,128]{1,0:T(8,128)S(1)}, u32[]{:S(2)}, u32[]{:S(2)}) %collective-permute-start.2) | collective-permute-done | bytes 200736 | tf_op jit(solution)/shard_map/ppermute | solution.py:453
  13.6 0.0 collective-permute-done.3.r3_ref
  13.6 0.0 copy-done
  13.6 0.0 copy-done.4
  13.6 2.3 %faces.1 = f32[1536,128]{1,0:T(8,128)} custom-call(s32[1,128]{1,0:T(1,128)S(1)} %bitcast.11, f32[192,768]{1,0:T(8,128)S(1)} %get-tuple-element.31.jump_ref, f32[192,768]{1,0:T(8,128)S(1)} %get-tuple-element.32.part_ref, f32[6,8,128]{2,1,0:T(8,128)S(1)} %get-tuple-element.33.aux_ref, bf16[512,768]{1,0:T(8,128)(2,1)S(1)} %get-tuple-element.34.hot_ref, ...), custom_call_target="tpu_custom_call" | custom-call | tf_op jit(solution)/shard_map/faces/pallas_call | solution.py:512
Async XLA Ops:
  0.0 9.1 %copy-start.1 = (f32[64,128]{1,0:T(8,128)S(1)}, f32[64,128]{1,0:T(8,128)}, u32[]{:S(2)}) copy-start(f32[64,128]{1,0:T(8,128)} %constant.12.clone.mab_ref) | copy-start | bytes 98308
  0.0 9.1 %copy-start.3 = (s32[1,1,6,128]{3,1,2,0:T(1,128)S(1)}, s32[1,1,6,128]{3,1,2,0:T(1,128)}, u32[]{:S(2)}) copy-start(s32[1,1,6,128]{3,1,2,0:T(1,128)} %param.16) | copy-start | bytes 9220
  0.0 9.1 %copy-start.2 = (s32[1,1,6,128]{3,1,2,0:T(1,128)S(1)}, s32[1,1,6,128]{3,1,2,0:T(1,128)}, u32[]{:S(2)}) copy-start(s32[1,1,6,128]{3,1,2,0:T(1,128)} %param.15) | copy-start | bytes 9220
  3.4 9.3 %collective-permute-start = (f32[392,128]{1,0:T(8,128)S(1)}, f32[392,128]{1,0:T(8,128)S(1)}, u32[]{:S(2)}, u32[]{:S(2)}) collective-permute-start(f32[392,128]{1,0:T(8,128)S(1)} %get-tuple-element.36), channel_id=1, source_target_pairs={{0,1},{1,0},{2,3},{3,2},{4,5},{5,4},{6,7},{7,6},{8,9},{9,8},{10,11... | collective-permute-start | bytes 602120 | tf_op jit(solution)/shard_map/ppermute | solution.py:453
  4.0 8.7 %collective-permute-start.1 = (f32[392,128]{1,0:T(8,128)S(1)}, f32[392,128]{1,0:T(8,128)S(1)}, u32[]{:S(2)}, u32[]{:S(2)}) collective-permute-start(f32[392,128]{1,0:T(8,128)S(1)} %get-tuple-element.37), channel_id=1, source_target_pairs={{0,7},{1,2},{2,1},{3,4},{4,3},{5,6},{6,5},{7,0},{8,15},{9,10},{10,... | collective-permute-start | bytes 602120 | tf_op jit(solution)/shard_map/ppermute | solution.py:453
  7.5 6.0 %collective-permute-start.2 = (f32[392,128]{1,0:T(8,128)S(1)}, f32[392,128]{1,0:T(8,128)S(1)}, u32[]{:S(2)}, u32[]{:S(2)}) collective-permute-start(f32[392,128]{1,0:T(8,128)S(1)} %get-tuple-element.38), channel_id=1, source_target_pairs={{0,8},{1,9},{2,10},{3,11},{4,12},{5,13},{6,14},{7,15},{8,0},{9,1},... | collective-permute-start | bytes 602120 | tf_op jit(solution)/shard_map/ppermute | solution.py:453
  9.1 4.4 %collective-permute-start.3 = (f32[392,128]{1,0:T(8,128)S(1)}, f32[392,128]{1,0:T(8,128)S(1)}, u32[]{:S(2)}, u32[]{:S(2)}) collective-permute-start(f32[392,128]{1,0:T(8,128)S(1)} %get-tuple-element.39), channel_id=1, source_target_pairs={{0,1},{1,0},{2,3},{3,2},{4,5},{5,4},{6,7},{7,6},{8,16},{9,17},{10,... | collective-permute-start | bytes 602120 | tf_op jit(solution)/shard_map/ppermute | solution.py:453
  9.1 4.4 %copy-start = (bf16[512,256]{1,0:T(8,128)(2,1)S(1)}, bf16[512,256]{1,0:T(8,128)(2,1)}, u32[]{:S(2)}) copy-start(bf16[512,256]{1,0:T(8,128)(2,1)} %constant.17.clone.zlift_ref) | copy-start | bytes 786436
  9.2 4.4 %copy-start.4 = (s32[1,1,128]{2,1,0:T(1,128)S(1)}, s32[1,1,128]{2,1,0:T(1,128)}, u32[]{:S(2)}) copy-start(s32[1,1,128]{2,1,0:T(1,128)} %param.12) | copy-start | bytes 1540
